TPU v7x, 128 devices: a whole 4x4x4 slice. The times are simulated.
128 devices in a mesh: dp: 128 (over y, z, x, core).
Axes of the slice: x: 4, y: 4, z: 4, core: 2. Of those that a mesh axis runs over, the one named last changes fastest.
Arguments:
- events: bfloat16 [131072, 512], P('dp'), may hold values from -6 to 6
- home_slot: int32 [131072], P('dp'), may hold values from 0 to 1024, as said below
- dest_slot: int32 [131072], P('dp'), may hold values from 0 to 1024, as said below
- seq_lens: int32 [256], P('dp'), may hold values from 0 to 1024, as said below
- weights: bfloat16 [512, 2560], replicated, may hold values from -0.25 to 0.25
- out_grad: bfloat16 [131072, 512], P('dp'), may hold values from -6 to 6
- momentum_in: float32 [512, 2048], P('dp'), may hold values from -3 to 3
- momentum_out: float32 [512, 512], P('dp'), may hold values from -3 to 3
Outputs:
- event_grad: bfloat16 [131072, 512], P('dp')
- new_momentum_in: float32 [512, 2048], P('dp')
- new_momentum_out: float32 [512, 512], P('dp')
Inputs may be any that keep to these rules, and one draw needn't show every extreme that they name: `seq_lens`: each device's 2 entries are the lengths of the sequences placed on it, in order, then zeros; the sequences' blocks, ceil(length / 512) each, add up to at most 2. `dest_slot`: for each row of a device's blocks: 1024 if the row lies in no sequence, else s * 8 + k, where s is the device that holds the row's event at home and k its slot among the rows that s sends to this device; no value below 1024 repeats on a device. `home_slot`: for each home row: 1024 if no sequence uses it, else t * 8 + k, where t is the device that takes the row and k its slot as in dest_slot; no value below 1024 repeats on a device, and the two arrays name the same rows. A device sends at most 8 rows to one device, and in every draw some device receives 8 rows from every device.
All inputs are finite; a program needn't handle non-finite values.
Results may differ from a plain program's by a relative error of at most 0.0085.
Values may be sent and summed in bfloat16 or wider, within the bound.
No kernel may reach another device: no remote copies, remote signals or barrier semaphores. Data moves between devices by JAX's collectives and lax.ppermute only.
A program may use at most 128 MiB of HBM per device.

v0:
```python
import functools

import jax
import jax.numpy as jnp
from jax import lax
from jax.experimental import pallas as pl
from jax.experimental.pallas import tpu as pltpu
from jax.sharding import Mesh
from jax.sharding import PartitionSpec as P

BLK = 512
DP = ("dp_0", "dp_1", "dp_2", "dp_3")
CHIPS = DP[:3]
CORE = DP[3]

NORM_EPS = 1e-05
DECAY = 0.9
TILE = 256
BF = jnp.bfloat16
F32 = jnp.float32


def dot(a, b):
    return jnp.dot(a, b, preferred_element_type=F32)


def dot_nt(a, b):
    return lax.dot_general(a, b, (((1,), (1,)), ((), ())), preferred_element_type=F32)


def dot_tn(a, b):
    return lax.dot_general(a, b, (((0,), (0,)), ((), ())), preferred_element_type=F32)


def rows_at(i):
    return pl.ds(pl.multiple_of(i * TILE, TILE), TILE)


def slot_rows(slots, first, count):
    places = lax.broadcasted_iota(jnp.int32, (count, slots.shape[1]), 0) + first
    return jnp.where(slots == places, 1.0, 0.0).astype(BF)


def slot_columns(spread, count):
    lane = lax.broadcasted_iota(jnp.int32, spread.shape, 1)
    parts = [
        jnp.where(spread == lane + at, 1.0, 0.0).astype(BF) for at in range(0, count, 128)
    ]
    return jnp.concatenate(parts, axis=1)


def spread_slots(slots):
    return jnp.transpose(jnp.broadcast_to(slots, (128, slots.shape[1])))


def place_kernel(slots_ref, rows_ref, out_ref):
    @pl.loop(0, out_ref.shape[0] // TILE)
    def _(i):
        pick = slot_rows(slots_ref[...], i * TILE, TILE)
        out_ref[rows_at(i), :] = dot(pick, rows_ref[...]).astype(BF)


def fetch_kernel(slots_ref, rows_ref, out_ref, spread_ref):
    spread_ref[...] = spread_slots(slots_ref[...])

    @pl.loop(0, out_ref.shape[0] // TILE)
    def _(i):
        pick = slot_columns(spread_ref[rows_at(i), :], rows_ref.shape[0])
        out_ref[rows_at(i), :] = dot(pick, rows_ref[...]).astype(BF)


def silu_parts(half):
    plus = 1.0 + jnp.tanh(half)
    value = half * plus
    return value, plus + value * (2.0 - plus)


def two_heads(rows):
    lane = lax.broadcasted_iota(jnp.int32, rows.shape, 1)
    none = jnp.zeros_like(rows)
    low = lane < 64
    return jnp.concatenate([jnp.where(low, rows, none), jnp.where(low, none, rows)], axis=0)


def own_lanes(stacked):
    half = stacked.shape[0] // 2
    lane = lax.broadcasted_iota(jnp.int32, (half, stacked.shape[1]), 1)
    return jnp.where(lane < 64, stacked[:half], stacked[half:])


def layer_kernel(
    lens_ref,
    dest_ref,
    inbox_ref,
    weights_ref,
    upstream_ref,
    sendback_ref,
    grads_ref,
    spread_ref,
    tokens_t,
    slope,
    gate,
    vals,
    queries,
    keys,
    attended,
    mixed_t,
    att_grad,
    near_w,
    near_d,
    far_w,
    far_d,
    key_sum,
    val_sum,
    hidden_grad,
    token_grad,
):
    row_count, width = inbox_ref.shape
    tiles = row_count // TILE
    pairs = width // 128
    first, second = lens_ref[0], lens_ref[1]
    joined = jnp.where(first > 0, first, second) > BLK
    spread_ref[...] = spread_slots(dest_ref[...])

    @pl.loop(0, tiles)
    def _(i):
        rows = rows_at(i)
        pick = slot_columns(spread_ref[rows, :], row_count)
        tokens = dot(pick, inbox_ref[...]).astype(BF)
        tokens_t[:, rows] = tokens.T
        for g in range(4):
            columns = slice(g * width, (g + 1) * width)
            half = dot(tokens, weights_ref[:, columns]) * 0.5
            value, slope2 = silu_parts(half)
            slope[rows, columns] = 0.5 * slope2
            if g == 0:
                gate[rows, :] = value
            elif g == 1:
                vals[rows, :] = value.astype(BF)
            elif g == 2:
                queries[rows, :] = value.astype(BF) * jnp.asarray(0.0625, BF)
            else:
                keys[rows, :] = value.astype(BF)

    @pl.loop(0, pairs)
    def _(p):
        lanes = pl.ds(pl.multiple_of(p * 128, 128), 128)
        for i in range(tiles):
            rows = slice(i * TILE, (i + 1) * TILE)
            stacked = two_heads(queries[rows, lanes])
            low, high = (i * TILE) // BLK * BLK, (i + 1) * TILE
            span = high - low
            weight, slope2 = silu_parts(dot_nt(stacked, keys[low:high, lanes]))
            place = lax.broadcasted_iota(jnp.int32, (TILE, span), 0) + (i * TILE - low)
            seen = lax.broadcasted_iota(jnp.int32, (TILE, span), 1) <= place
            seen = jnp.concatenate([seen, seen], axis=0)
            weight = jnp.where(seen, weight, 0.0).astype(BF)
            near_w[p, i, :, :span] = weight
            near_d[p, i, :, :span] = jnp.where(seen, slope2, 0.0).astype(BF)
            attended[rows, lanes] = own_lanes(dot(weight, vals[low:high, lanes]))
            if low > 0:

                @pl.when(joined)
                def _(i=i, rows=rows, stacked=stacked, low=low):
                    weight, slope2 = silu_parts(dot_nt(stacked, keys[:low, lanes]))
                    weight = weight.astype(BF)
                    j = i - low // TILE
                    far_w[p, j] = weight
                    far_d[p, j] = slope2.astype(BF)
                    attended[rows, lanes] += own_lanes(dot(weight, vals[:low, lanes]))

    @pl.loop(0, tiles)
    def _(i):
        rows = rows_at(i)
        value = attended[rows, :]
        centre = jnp.mean(value, axis=1, keepdims=True)
        centred = value - centre
        spread = jnp.mean(centred * centred, axis=1, keepdims=True)
        scale = lax.rsqrt(spread + NORM_EPS)
        normed = centred * scale
        gates = gate[rows, :]
        mixed_t[:, rows] = (normed * gates).astype(BF).T
        mixed_grad = dot_nt(upstream_ref[rows, :], weights_ref[:, 4 * width :])
        hidden_grad[rows, :width] = (mixed_grad * normed * slope[rows, :width]).astype(BF)
        down = mixed_grad * gates
        mean_down = jnp.mean(down, axis=1, keepdims=True)
        mean_both = jnp.mean(down * normed, axis=1, keepdims=True)
        att_grad[rows, :] = (scale * (down - mean_down - normed * mean_both)).astype(BF)

    @pl.loop(0, pairs)
    def _(p):
        start = pl.multiple_of(p * 128, 128)
        lanes = pl.ds(start, 128)
        key_sum[...] = jnp.zeros_like(key_sum)
        val_sum[...] = jnp.zeros_like(val_sum)
        query_lanes = pl.ds(pl.multiple_of(start + 2 * width, 128), 128)
        for i in range(tiles):
            rows = slice(i * TILE, (i + 1) * TILE)
            stacked = two_heads(queries[rows, lanes])
            down = two_heads(att_grad[rows, lanes])
            low, high = (i * TILE) // BLK * BLK, (i + 1) * TILE
            span = high - low
            score = dot_nt(down, vals[low:high, lanes]).astype(BF) * near_d[p, i, :, :span]
            val_sum[low:high] += dot_tn(near_w[p, i, :, :span], down)
            key_sum[low:high] += dot_tn(score, stacked)
            attended[rows, :128] = own_lanes(dot(score, keys[low:high, lanes]))
            if low > 0:

                @pl.when(joined)
                def _(i=i, rows=rows, stacked=stacked, down=down, low=low):
                    j = i - low // TILE
                    score = dot_nt(down, vals[:low, lanes]).astype(BF) * far_d[p, j]
                    val_sum[:low] += dot_tn(far_w[p, j], down)
                    key_sum[:low] += dot_tn(score, stacked)
                    attended[rows, :128] += own_lanes(dot(score, keys[:low, lanes]))

        for source, group, factor in ((val_sum, 1, 1.0), (attended, 2, 0.0625), (key_sum, 3, 1.0)):
            columns = pl.ds(pl.multiple_of(start + group * width, 128), 128)
            rounded = (source[:, :128] * factor).astype(BF).astype(F32)
            hidden_grad[:, columns] = (rounded * slope[:, columns]).astype(BF)

    @pl.loop(0, tiles)
    def _(i):
        rows = rows_at(i)
        total = dot_nt(hidden_grad[rows, :], weights_ref[:, : 4 * width])
        token_grad[rows, :] = (upstream_ref[rows, :].astype(F32) + total).astype(BF)

    @pl.loop(0, tiles)
    def _(i):
        pick = slot_rows(dest_ref[...], i * TILE, TILE)
        sendback_ref[rows_at(i), :] = dot(pick, token_grad[...]).astype(BF)

    @pl.loop(0, 4 * width // TILE)
    def _(i):
        columns = rows_at(i)
        grads_ref[:, columns] = dot(tokens_t[...], hidden_grad[:, columns]).astype(BF)

    grads_ref[:, 4 * width :] = dot(mixed_t[...], upstream_ref[...]).astype(BF)


VMEM_SPEC = pl.BlockSpec(memory_space=pltpu.VMEM)
SMEM_SPEC = pl.BlockSpec(memory_space=pltpu.SMEM)


def place(slots, rows):
    count, width = rows.shape
    return pl.pallas_call(
        place_kernel,
        name="place_rows",
        out_shape=jax.ShapeDtypeStruct((count, width), BF),
        in_specs=[VMEM_SPEC] * 2,
        out_specs=VMEM_SPEC,
        cost_estimate=pl.CostEstimate(
            flops=2 * count * count * width, bytes_accessed=4 * count * width, transcendentals=0
        ),
    )(slots, rows)


def fetch(slots, rows):
    count, width = rows.shape
    return pl.pallas_call(
        fetch_kernel,
        name="fetch_rows",
        out_shape=jax.ShapeDtypeStruct((count, width), BF),
        in_specs=[VMEM_SPEC] * 2,
        out_specs=VMEM_SPEC,
        scratch_shapes=[pltpu.VMEM((count, 128), jnp.int32)],
        cost_estimate=pl.CostEstimate(
            flops=2 * count * count * width, bytes_accessed=4 * count * width, transcendentals=0
        ),
    )(slots, rows)


def layer(lens, dest, inbox, weights, upstream):
    count, width = inbox.shape
    tiles, pairs, far = count // TILE, width // 128, (count - BLK) // TILE
    return pl.pallas_call(
        layer_kernel,
        name="layer_step",
        out_shape=(
            jax.ShapeDtypeStruct((count, width), BF),
            jax.ShapeDtypeStruct(weights.shape, BF),
        ),
        in_specs=[SMEM_SPEC] + [VMEM_SPEC] * 4,
        out_specs=(VMEM_SPEC, VMEM_SPEC),
        scratch_shapes=[
            pltpu.VMEM((count, 128), jnp.int32),
            pltpu.VMEM((width, count), BF),
            pltpu.VMEM((count, 4 * width), F32),
            pltpu.VMEM((count, width), F32),
            pltpu.VMEM((count, width), BF),
            pltpu.VMEM((count, width), BF),
            pltpu.VMEM((count, width), BF),
            pltpu.VMEM((count, width), F32),
            pltpu.VMEM((width, count), BF),
            pltpu.VMEM((count, width), BF),
            pltpu.VMEM((pairs, tiles, 2 * TILE, BLK), BF),
            pltpu.VMEM((pairs, tiles, 2 * TILE, BLK), BF),
            pltpu.VMEM((pairs, far, 2 * TILE, BLK), BF),
            pltpu.VMEM((pairs, far, 2 * TILE, BLK), BF),
            pltpu.VMEM((count, 128), F32),
            pltpu.VMEM((count, 128), F32),
            pltpu.VMEM((count, 4 * width), BF),
            pltpu.VMEM((count, width), BF),
        ],
        compiler_params=pltpu.CompilerParams(vmem_limit_bytes=60 << 20),
        cost_estimate=pl.CostEstimate(
            flops=30_000_000_000, bytes_accessed=12_000_000, transcendentals=10_000_000
        ),
    )(lens, dest, inbox, weights, upstream)


def core_swap(value):
    return lax.ppermute(value, CORE, [(0, 1), (1, 0)])


def summed_rows(grads):
    rows, columns = grads.shape
    chips = lax.axis_size(CHIPS)
    half = columns // 2
    core = lax.axis_index(CORE)
    mine = lax.dynamic_slice_in_dim(grads, core * half, half, axis=1)
    other = lax.dynamic_slice_in_dim(grads, (1 - core) * half, half, axis=1)
    both = (mine.astype(F32) + core_swap(other).astype(F32)).astype(BF)
    spread = both.reshape(chips, rows // chips, half)
    arrived = lax.all_to_all(spread, CHIPS, split_axis=0, concat_axis=0, tiled=True)
    total = arrived.astype(F32).sum(axis=0)
    keep = rows // chips // 2
    mine = lax.dynamic_slice_in_dim(total, core * keep, keep, axis=0)
    other = core_swap(lax.dynamic_slice_in_dim(total, (1 - core) * keep, keep, axis=0))
    return jnp.where(
        core == 0,
        jnp.concatenate([mine, other], axis=1),
        jnp.concatenate([other, mine], axis=1),
    )


def shards(events, home_slot, dest_slot, seq_lens, weights, out_grad, momentum_in, momentum_out):
    row_count, model_width = events.shape
    home = home_slot.reshape(1, row_count)
    dest = dest_slot.reshape(1, row_count)
    peers = lax.axis_size(DP)

    def exchange(rows):
        blocks = rows.reshape(peers, row_count // peers, model_width)
        arrived = lax.all_to_all(blocks, DP, split_axis=0, concat_axis=0, tiled=True)
        return arrived.reshape(row_count, model_width)

    inbox = exchange(place(home, events))
    sendback, grads = layer(seq_lens, dest, inbox, weights, out_grad)
    event_grad = fetch(home, exchange(sendback))
    total = summed_rows(grads)
    grad_scale = (peers * row_count) ** (-0.5)
    return (
        event_grad,
        DECAY * momentum_in + grad_scale * total[:, : 4 * model_width],
        DECAY * momentum_out + grad_scale * total[:, 4 * model_width :],
    )


def solution(mesh):
    split = Mesh(mesh.devices.reshape(4, 4, 4, 2), DP)
    return jax.shard_map(
        shards,
        mesh=split,
        in_specs=(P(DP, None), P(DP), P(DP), P(DP), P(), P(DP, None), P(DP, None), P(DP, None)),
        out_specs=(P(DP, None), P(DP, None), P(DP, None)),
        check_vma=False,
    )
```

profile of v0, /device:TPU:1, one launch (start us, length us, event | category | flops | bytes accessed | tf_op | source)
XLA Modules:
  0.0 150.0 jit_solution(12702254421265731295)
XLA Ops:
  0.6 4.0 %place_rows.1 = bf16[1024,512]{1,0:T(8,128)(2,1)} custom-call(s32[1,1024]{1,0:T(1,128)} %bitcast.12, bf16[1024,512]{1,0:T(8,128)(2,1)} %rows_ref.1), custom_call_target="tpu_custom_call" | custom-call | flops 1073741824 | bytes 2097152 | tf_op jit(solution)/shard_map/place_rows/pallas_call | solution.py:247
  4.6 11.5 %all-to-all-start = ((bf16[128,8,512]{2,1,0:T(8,128)(2,1)}), bf16[128,8,512]{2,1,0:T(8,128)(2,1)S(1)}, u32[]{:S(2)}, u32[]{:S(2)}) async-start(bf16[128,8,512]{2,1,0:T(8,128)(2,1)} %bitcast.10), calls=%async_computation | async-start | bytes 2097152 | tf_op jit(solution)/shard_map/all_to_all | solution.py:346
  16.1 19.3 %all-to-all-done = bf16[128,8,512]{2,1,0:T(8,128)(2,1)S(1)} async-done(((bf16[128,8,512]{2,1,0:T(8,128)(2,1)}), bf16[128,8,512]{2,1,0:T(8,128)(2,1)S(1)}, u32[]{:S(2)}, u32[]{:S(2)}) %all-to-all-start) | async-done | bytes 1048608 | tf_op jit(solution)/shard_map/all_to_all | solution.py:346
  35.4 0.0 copy-start.2
  35.4 1.0 copy-done.2
  36.4 37.3 %layer_step.1 = (bf16[1024,512]{1,0:T(8,128)(2,1)}, bf16[512,2560]{1,0:T(8,128)(2,1)}) custom-call(s32[2]{0:T(128)} %lens_ref.1, s32[1,1024]{1,0:T(1,128)} %bitcast.11, bf16[1024,512]{1,0:T(8,128)(2,1)} %bitcast.9, bf16[512,2560]{1,0:T(8,128)(2,1)} %weights_ref.1, bf16[1024,512]{1,0:T(8,128)(2,1)} %upstream_ref.1), custom_call_target="tpu_custom_call" | custom-call | flops 30000001024 | bytes 12000000 | tf_op jit(solution)/shard_map/layer_step/pallas_call | solution.py:277
  73.7 0.0 copy-start
  73.7 2.6 %constant_dynamic-slice_fusion.2 = bf16[512,1280]{1,0:T(8,128)(2,1)} fusion(bf16[512,2560]{1,0:T(8,128)(2,1)} %get-tuple-element.6, s32[]{:T(128)S(6)} %select_n.22), kind=kLoop, calls=%fused_computation.10 | loop fusion | bytes 2621444 | tf_op jit(solution)/shard_map/dynamic_slice | solution.py:323
  76.3 0.9 collective-permute-start
  77.2 3.0 %collective-permute-done = bf16[512,1280]{1,0:T(8,128)(2,1)} collective-permute-done((bf16[512,1280]{1,0:T(8,128)(2,1)}, bf16[512,1280]{1,0:T(8,128)(2,1)}, u32[]{:S(2)}, u32[]{:S(2)}) %collective-permute-start) | collective-permute-done | bytes 1310752 | tf_op jit(solution)/shard_map/ppermute | solution.py:314
  80.2 0.0 copy-done
  80.2 1.6 %fusion = bf16[64,8,1280]{2,1,0:T(8,128)(2,1)S(1)} fusion(bf16[512,1280]{1,0:T(8,128)(2,1)} %collective-permute-done, bf16[512,2560]{1,0:T(8,128)(2,1)S(1)} %copy-done, s32[]{:T(128)S(6)} %select_n.21), kind=kLoop, calls=%fused_computation.2 | loop fusion | flops 2621440 | bytes 3932164 | tf_op jit(solution)/shard_map/reshape | solution.py:325
  81.8 36.9 %all_to_all.15 = bf16[64,8,1280]{2,1,0:T(8,128)(2,1)S(1)} all-to-all(bf16[64,8,1280]{2,1,0:T(8,128)(2,1)S(1)} %fusion), channel_id=1, replica_groups=mesh['dp_0'=4,'dp_1'=4,'dp_2'=4,'dp_3'=2] {'dp_0','dp_1','dp_2'}, dimensions={0} | all-to-all | bytes 2621440 | tf_op jit(solution)/shard_map/all_to_all | solution.py:326
  118.8 5.3 %all-to-all-start.1 = ((bf16[128,8,512]{2,1,0:T(8,128)(2,1)}), bf16[128,8,512]{2,1,0:T(8,128)(2,1)S(1)}, u32[]{:S(2)}, u32[]{:S(2)}) async-start(bf16[128,8,512]{2,1,0:T(8,128)(2,1)} %bitcast.4), calls=%async_computation.1 | async-start | bytes 2097152 | tf_op jit(solution)/shard_map/all_to_all | solution.py:346
  124.1 0.2 convert_reduce_fusion
  124.3 1.3 collective-permute-start.1
  125.6 18.0 %all-to-all-done.1 = bf16[128,8,512]{2,1,0:T(8,128)(2,1)S(1)} async-done(((bf16[128,8,512]{2,1,0:T(8,128)(2,1)}), bf16[128,8,512]{2,1,0:T(8,128)(2,1)S(1)}, u32[]{:S(2)}, u32[]{:S(2)}) %all-to-all-start.1) | async-done | bytes 1048608 | tf_op jit(solution)/shard_map/all_to_all | solution.py:346
  143.5 0.0 copy-start.1
  143.5 1.0 copy-done.1
  144.5 0.0 copy-start.3
  144.5 0.0 copy-start.4
  144.5 4.2 %fetch_rows.1 = bf16[1024,512]{1,0:T(8,128)(2,1)} custom-call(s32[1,1024]{1,0:T(1,128)} %bitcast.13, bf16[1024,512]{1,0:T(8,128)(2,1)} %bitcast.8), custom_call_target="tpu_custom_call" | custom-call | flops 1073741824 | bytes 2097152 | tf_op jit(solution)/shard_map/fetch_rows/pallas_call | solution.py:261
  148.7 0.0 collective-permute-done.1
  148.7 0.0 copy-done.3
  148.7 0.6 fusion.1
  149.4 0.0 copy-done.4
  149.4 0.6 fusion.2
  (2 shorter events, 0.0 us)
Async XLA Ops:
  4.6 30.8 %all-to-all-start = ((bf16[128,8,512]{2,1,0:T(8,128)(2,1)}), bf16[128,8,512]{2,1,0:T(8,128)(2,1)S(1)}, u32[]{:S(2)}, u32[]{:S(2)}) async-start(bf16[128,8,512]{2,1,0:T(8,128)(2,1)} %bitcast.10), calls=%async_computation | async-start | bytes 2097152 | tf_op jit(solution)/shard_map/all_to_all | solution.py:346
  35.4 1.0 copy-start.2
  73.7 6.5 %copy-start = (bf16[512,2560]{1,0:T(8,128)(2,1)S(1)}, bf16[512,2560]{1,0:T(8,128)(2,1)}, u32[]{:S(2)}) copy-start(bf16[512,2560]{1,0:T(8,128)(2,1)} %get-tuple-element.6) | copy-start | bytes 7864324
  76.3 3.9 %collective-permute-start = (bf16[512,1280]{1,0:T(8,128)(2,1)}, bf16[512,1280]{1,0:T(8,128)(2,1)}, u32[]{:S(2)}, u32[]{:S(2)}) collective-permute-start(bf16[512,1280]{1,0:T(8,128)(2,1)} %constant_dynamic-slice_fusion.2), channel_id=1, source_target_pairs={{0,1},{1,0},{2,3},{3,2},{4,5},{5,4},{6,7},{7,6},{8,9},{9,8},{10,11... | collective-permute-start | bytes 3932168 | tf_op jit(solution)/shard_map/ppermute | solution.py:314
  118.8 24.8 %all-to-all-start.1 = ((bf16[128,8,512]{2,1,0:T(8,128)(2,1)}), bf16[128,8,512]{2,1,0:T(8,128)(2,1)S(1)}, u32[]{:S(2)}, u32[]{:S(2)}) async-start(bf16[128,8,512]{2,1,0:T(8,128)(2,1)} %bitcast.4), calls=%async_computation.1 | async-start | bytes 2097152 | tf_op jit(solution)/shard_map/all_to_all | solution.py:346
  124.3 24.4 %collective-permute-start.1 = (f32[4,1280]{1,0:T(4,128)S(1)}, f32[4,1280]{1,0:T(4,128)S(1)}, u32[]{:S(2)}, u32[]{:S(2)}) collective-permute-start(f32[4,1280]{1,0:T(4,128)S(1)} %get-tuple-element.8), channel_id=1, source_target_pairs={{0,1},{1,0},{2,3},{3,2},{4,5},{5,4},{6,7},{7,6},{8,9},{9,8},{10,11... | collective-permute-start | bytes 61448 | tf_op jit(solution)/shard_map/ppermute | solution.py:314
  143.5 1.0 copy-start.1
  144.5 4.2 %copy-start.3 = (f32[4,2048]{1,0:T(4,128)S(1)}, f32[4,2048]{1,0:T(4,128)}, u32[]{:S(2)}) copy-start(f32[4,2048]{1,0:T(4,128)} %param.14) | copy-start | bytes 98308
  144.5 4.8 %copy-start.4 = (f32[4,512]{1,0:T(4,128)S(1)}, f32[4,512]{1,0:T(4,128)}, u32[]{:S(2)}) copy-start(f32[4,512]{1,0:T(4,128)} %param.15) | copy-start | bytes 24580
where the time goes:
time: 150 us
  Pallas kernels  45.5 us (30%)
  waiting for transfers between devices  40.3 us (27%)
  blocking collectives  36.9 us (25%)
  starting transfers between devices  18.9 us (13%)
  local copies, waits for them, and re-layouts  4.56 us (3%)
  other arithmetic  3.08 us (2%)
    pallas_call x1, Pallas kernels, layer(): pl.pallas_call(layer_kernel, name='layer_step', out_shape=(jax.ShapeDtype...  37.3 us
    all_to_all x2, waiting for transfers between devices, exchange(): lax.all_to_all(blocks, DP, split_axis=0, concat_axis=0, tiled=True)  37.3 us
    all_to_all x1, blocking collectives, summed_rows(): lax.all_to_all(spread, CHIPS, split_axis=0, concat_axis=0, tiled=True)  36.9 us
    all_to_all x2, starting transfers between devices, exchange(): lax.all_to_all(blocks, DP, split_axis=0, concat_axis=0, tiled=True)  16.8 us
    pallas_call x1, Pallas kernels, fetch(): pl.pallas_call(fetch_kernel, name='fetch_rows', out_shape=jax.ShapeDtypeS...  4.17 us
    pallas_call x1, Pallas kernels, place(): pl.pallas_call(place_kernel, name='place_rows', out_shape=jax.ShapeDtypeS...  3.96 us
    ppermute x2, waiting for transfers between devices, core_swap(): return lax.ppermute(value, CORE, [(0, 1), (1, 0)])  3.01 us
  transfers between devices with their start and end apart: 4, of which 3 were waited for; matrix products, arithmetic and copies ran while one was open for 0% of the time, Pallas kernels for 3%

commit v1 on v0

--- a/solution.py
+++ b/solution.py
@@ -60,15 +60,6 @@
         out_ref[rows_at(i), :] = dot(pick, rows_ref[...]).astype(BF)
 
 
-def fetch_kernel(slots_ref, rows_ref, out_ref, spread_ref):
-    spread_ref[...] = spread_slots(slots_ref[...])
-
-    @pl.loop(0, out_ref.shape[0] // TILE)
-    def _(i):
-        pick = slot_columns(spread_ref[rows_at(i), :], rows_ref.shape[0])
-        out_ref[rows_at(i), :] = dot(pick, rows_ref[...]).astype(BF)
-
-
 def silu_parts(half):
     plus = 1.0 + jnp.tanh(half)
     value = half * plus
@@ -95,7 +86,8 @@
     weights_ref,
     upstream_ref,
     sendback_ref,
-    grads_ref,
+    kept_ref,
+    given_ref,
     spread_ref,
     tokens_t,
     slope,
@@ -230,12 +222,70 @@
         pick = slot_rows(dest_ref[...], i * TILE, TILE)
         sendback_ref[rows_at(i), :] = dot(pick, token_grad[...]).astype(BF)
 
-    @pl.loop(0, 4 * width // TILE)
-    def _(i):
-        columns = rows_at(i)
-        grads_ref[:, columns] = dot(tokens_t[...], hidden_grad[:, columns]).astype(BF)
-
-    grads_ref[:, 4 * width :] = dot(mixed_t[...], upstream_ref[...]).astype(BF)
+    halves = kept_ref.shape[1] // TILE
+    ours = lax.axis_index(CORE)
+
+    def put(value, i):
+        half = i // halves
+        columns = rows_at(i - half * halves)
+
+        @pl.when(half == ours)
+        def _():
+            kept_ref[:, columns] = value
+
+        @pl.when(half != ours)
+        def _():
+            given_ref[:, columns] = value
+
+    inner = 4 * width // TILE
+
+    @pl.loop(0, inner)
+    def _(i):
+        put(dot(tokens_t[...], hidden_grad[:, rows_at(i)]).astype(BF), i)
+
+    for i in range(width // TILE):
+        columns = slice(i * TILE, (i + 1) * TILE)
+        put(dot(mixed_t[...], upstream_ref[:, columns]).astype(BF), inner + i)
+
+
+def pack_kernel(rows_ref, kept_ref, got_ref, out_ref):
+    peers, slots, width = rows_ref.shape
+    half = kept_ref.shape[1] // 2
+    out_ref[:, :, :width] = rows_ref[...]
+    both = (kept_ref[...].astype(F32) + got_ref[...].astype(F32)).reshape(peers // 2, 8, 2 * half)
+    turned = pltpu.roll(both, 4, 1)
+    upper = lax.broadcasted_iota(jnp.int32, (peers // 2, 8, half), 1) < 4
+    even = jnp.where(upper, both[:, :, :half], turned[:, :, half:])
+    odd = jnp.where(upper, turned[:, :, :half], both[:, :, half:])
+    joint = jnp.stack([even, odd], axis=1).reshape(peers, 8, half)
+    out_ref[:, :, width:] = joint.astype(BF)
+
+
+def finish_kernel(scale, slots_ref, arrived_ref, in_ref, out_ref, events_ref, new_in, new_out, spread_ref, rows_ref):
+    peers, slots, _ = arrived_ref.shape
+    count, width = events_ref.shape
+    spread_ref[...] = spread_slots(slots_ref[...])
+    rows_ref[...] = arrived_ref[:, :, :width].reshape(count, width)
+
+    @pl.loop(0, count // TILE)
+    def _(i):
+        pick = slot_columns(spread_ref[rows_at(i), :], count)
+        events_ref[rows_at(i), :] = dot(pick, rows_ref[...]).astype(BF)
+
+    part = arrived_ref.shape[2] - width
+
+    def add(i, sums):
+        return tuple(
+            total + arrived_ref[2 * i + core, :, width:].astype(F32) for core, total in enumerate(sums)
+        )
+
+    none = jnp.zeros((slots, part), F32)
+    sums = lax.fori_loop(0, peers // 2, add, (none, none))
+    pieces = [total[4 * h : 4 * h + 4] for total in sums for h in range(2)]
+    total = jnp.concatenate(pieces, axis=1) * scale
+    inner = in_ref.shape[1]
+    new_in[...] = DECAY * in_ref[...] + total[:, :inner]
+    new_out[...] = DECAY * out_ref[...] + total[:, inner:]
 
 
 VMEM_SPEC = pl.BlockSpec(memory_space=pltpu.VMEM)
@@ -256,19 +306,40 @@
     )(slots, rows)
 
 
-def fetch(slots, rows):
-    count, width = rows.shape
+def pack(rows, kept, got):
+    peers, slots, width = rows.shape
+    out = (peers, slots, width + kept.shape[1] // 2)
     return pl.pallas_call(
-        fetch_kernel,
-        name="fetch_rows",
-        out_shape=jax.ShapeDtypeStruct((count, width), BF),
-        in_specs=[VMEM_SPEC] * 2,
+        pack_kernel,
+        name="pack_rows",
+        out_shape=jax.ShapeDtypeStruct(out, BF),
+        in_specs=[VMEM_SPEC] * 3,
         out_specs=VMEM_SPEC,
-        scratch_shapes=[pltpu.VMEM((count, 128), jnp.int32)],
+        compiler_params=pltpu.CompilerParams(vmem_limit_bytes=32 << 20),
+        cost_estimate=pl.CostEstimate(
+            flops=kept.size, bytes_accessed=2 * 2 * (rows.size + kept.size), transcendentals=0
+        ),
+    )(rows, kept, got)
+
+
+def finish(scale, slots, arrived, momentum_in, momentum_out):
+    count, width = slots.shape[1], momentum_out.shape[1]
+    return pl.pallas_call(
+        functools.partial(finish_kernel, scale),
+        name="finish_step",
+        out_shape=(
+            jax.ShapeDtypeStruct((count, width), BF),
+            jax.ShapeDtypeStruct(momentum_in.shape, F32),
+            jax.ShapeDtypeStruct(momentum_out.shape, F32),
+        ),
+        in_specs=[VMEM_SPEC] * 4,
+        out_specs=(VMEM_SPEC,) * 3,
+        scratch_shapes=[pltpu.VMEM((count, 128), jnp.int32), pltpu.VMEM((count, width), BF)],
+        compiler_params=pltpu.CompilerParams(vmem_limit_bytes=32 << 20),
         cost_estimate=pl.CostEstimate(
             flops=2 * count * count * width, bytes_accessed=4 * count * width, transcendentals=0
         ),
-    )(slots, rows)
+    )(slots, arrived, momentum_in, momentum_out)
 
 
 def layer(lens, dest, inbox, weights, upstream):
@@ -279,10 +350,11 @@
         name="layer_step",
         out_shape=(
             jax.ShapeDtypeStruct((count, width), BF),
-            jax.ShapeDtypeStruct(weights.shape, BF),
+            jax.ShapeDtypeStruct((width, weights.shape[1] // 2), BF),
+            jax.ShapeDtypeStruct((width, weights.shape[1] // 2), BF),
         ),
         in_specs=[SMEM_SPEC] + [VMEM_SPEC] * 4,
-        out_specs=(VMEM_SPEC, VMEM_SPEC),
+        out_specs=(VMEM_SPEC,) * 3,
         scratch_shapes=[
             pltpu.VMEM((count, 128), jnp.int32),
             pltpu.VMEM((width, count), BF),
@@ -310,52 +382,23 @@
     )(lens, dest, inbox, weights, upstream)
 
 
-def core_swap(value):
-    return lax.ppermute(value, CORE, [(0, 1), (1, 0)])
-
-
-def summed_rows(grads):
-    rows, columns = grads.shape
-    chips = lax.axis_size(CHIPS)
-    half = columns // 2
-    core = lax.axis_index(CORE)
-    mine = lax.dynamic_slice_in_dim(grads, core * half, half, axis=1)
-    other = lax.dynamic_slice_in_dim(grads, (1 - core) * half, half, axis=1)
-    both = (mine.astype(F32) + core_swap(other).astype(F32)).astype(BF)
-    spread = both.reshape(chips, rows // chips, half)
-    arrived = lax.all_to_all(spread, CHIPS, split_axis=0, concat_axis=0, tiled=True)
-    total = arrived.astype(F32).sum(axis=0)
-    keep = rows // chips // 2
-    mine = lax.dynamic_slice_in_dim(total, core * keep, keep, axis=0)
-    other = core_swap(lax.dynamic_slice_in_dim(total, (1 - core) * keep, keep, axis=0))
-    return jnp.where(
-        core == 0,
-        jnp.concatenate([mine, other], axis=1),
-        jnp.concatenate([other, mine], axis=1),
-    )
-
-
 def shards(events, home_slot, dest_slot, seq_lens, weights, out_grad, momentum_in, momentum_out):
     row_count, model_width = events.shape
     home = home_slot.reshape(1, row_count)
     dest = dest_slot.reshape(1, row_count)
     peers = lax.axis_size(DP)
-
-    def exchange(rows):
-        blocks = rows.reshape(peers, row_count // peers, model_width)
-        arrived = lax.all_to_all(blocks, DP, split_axis=0, concat_axis=0, tiled=True)
-        return arrived.reshape(row_count, model_width)
-
-    inbox = exchange(place(home, events))
-    sendback, grads = layer(seq_lens, dest, inbox, weights, out_grad)
-    event_grad = fetch(home, exchange(sendback))
-    total = summed_rows(grads)
+    slots = row_count // peers
+
+    def exchange(blocks):
+        return lax.all_to_all(blocks, DP, split_axis=0, concat_axis=0, tiled=True)
+
+    outbox = place(home, events).reshape(peers, slots, model_width)
+    inbox = exchange(outbox).reshape(row_count, model_width)
+    sendback, kept, given = layer(seq_lens, dest, inbox, weights, out_grad)
+    got = lax.ppermute(given, CORE, [(0, 1), (1, 0)])
+    wire = pack(sendback.reshape(peers, slots, model_width), kept, got)
     grad_scale = (peers * row_count) ** (-0.5)
-    return (
-        event_grad,
-        DECAY * momentum_in + grad_scale * total[:, : 4 * model_width],
-        DECAY * momentum_out + grad_scale * total[:, 4 * model_width :],
-    )
+    return finish(grad_scale, home, exchange(wire), momentum_in, momentum_out)
 
 
 def solution(mesh):

time: 150 us -> 133 us (0.89)
  waiting for transfers between devices: 40.3 us -> 3.24 us
  blocking collectives: 36.9 us -> 67.8 us
  starting transfers between devices: 18.9 us -> 0.01 us
  Pallas kernels: 45.5 us -> 58.1 us
  other arithmetic: 3.08 us -> 0 us
  local copies, waits for them, and re-layouts: 4.56 us -> 2.56 us
    all_to_all x2 -> x0, waiting for transfers between devices: 37.3 us -> none  [exchange(): lax.all_to_all(blocks, DP, split_axis=0, concat_axis=0, tiled=True)]
    all_to_all x1 -> x2, blocking collectives: 36.9 us -> 67.8 us  [exchange(): return lax.all_to_all(blocks, DP, split_axis=0, concat_axis=0, tiled=True)]
    all_to_all x2 -> x0, starting transfers between devices: 16.8 us -> none  [exchange(): lax.all_to_all(blocks, DP, split_axis=0, concat_axis=0, tiled=True)]
    pallas_call x1, Pallas kernels: 37.3 us -> 50.2 us  [layer(): pl.pallas_call(layer_kernel, name='layer_step', out_shape=(jax.ShapeDtype...]
    dynamic_slice x2 -> x0, local copies, waits for them, and re-layouts: 2.61 us -> none  [the longest x1 2.6 us: summed_rows(): other = lax.dynamic_slice_in_dim(grads, (1 - core) * half, half, axis=1)]
    ppermute x2 -> x1, starting transfers between devices: 2.16 us -> 0.01 us  [shards(): got = lax.ppermute(given, CORE, [(0, 1), (1, 0)])]
    reshape x1 -> x0, other arithmetic: 1.63 us -> none  [summed_rows(): spread = both.reshape(chips, rows // chips, half)]
    pallas_call x1 -> x2, Pallas kernels: 4.17 us -> 3.93 us  [the longest x1 3.39 us: finish(): pl.pallas_call(functools.partial(finish_kernel, scale), name='finish_step...]
  transfers between devices with their start and end apart: 4 -> 1, of which waited for: 3 -> 1; matrix products, arithmetic and copies ran while one was open for 0% -> 0% of each run, Pallas kernels for 3% -> 0%
where the time goes in v1:
time: 133 us; the launch traced here: 132 us
  blocking collectives  67.8 us (51%)
  Pallas kernels  58.1 us (44%)
  waiting for transfers between devices  3.24 us (2%)
  local copies, waits for them, and re-layouts  2.56 us (2%)
    all_to_all x2, blocking collectives, exchange(): return lax.all_to_all(blocks, DP, split_axis=0, concat_axis=0, tiled=True)  67.8 us
    pallas_call x1, Pallas kernels, layer(): pl.pallas_call(layer_kernel, name='layer_step', out_shape=(jax.ShapeDtype...  50.2 us
    pallas_call x1, Pallas kernels, place(): pl.pallas_call(place_kernel, name='place_rows', out_shape=jax.ShapeDtypeS...  3.96 us
    pallas_call x1, Pallas kernels, finish(): pl.pallas_call(functools.partial(finish_kernel, scale), name='finish_step...  3.39 us
    ppermute x1, waiting for transfers between devices, shards(): got = lax.ppermute(given, CORE, [(0, 1), (1, 0)])  3.24 us
  transfers between devices with their start and end apart: 1, of which 1 were waited for; matrix products, arithmetic and copies ran while one was open for 0% of the time, Pallas kernels for 0%

profile of v1, /device:TPU:1, one launch (start us, length us, event | category | flops | bytes accessed | tf_op | source)
XLA Modules:
  0.0 132.3 jit_solution(17313875568192809373)
XLA Ops:
  0.6 4.0 %place_rows.1 = bf16[1024,512]{1,0:T(8,128)(2,1)} custom-call(s32[1,1024]{1,0:T(1,128)} %bitcast.6, bf16[1024,512]{1,0:T(8,128)(2,1)} %rows_ref.1), custom_call_target="tpu_custom_call" | custom-call | flops 1073741824 | bytes 2097152 | tf_op jit(solution)/shard_map/place_rows/pallas_call | solution.py:297
  4.6 31.0 %all_to_all.10 = bf16[128,8,512]{2,1,0:T(8,128)(2,1)} all-to-all(bf16[128,8,512]{2,1,0:T(8,128)(2,1)} %bitcast.9), channel_id=1, replica_groups=mesh['dp_0'=4,'dp_1'=4,'dp_2'=4,'dp_3'=2] {'dp_0','dp_1','dp_2','dp_3'}, dimensions={0} | all-to-all | bytes 2097152 | tf_op jit(solution)/shard_map/all_to_all | solution.py:393
  35.5 50.2 %layer_step.1 = (bf16[1024,512]{1,0:T(8,128)(2,1)}, bf16[512,1280]{1,0:T(8,128)(2,1)}, bf16[512,1280]{1,0:T(8,128)(2,1)}) custom-call(s32[2]{0:T(128)} %lens_ref.1, s32[1,1024]{1,0:T(1,128)} %bitcast.10, bf16[1024,512]{1,0:T(8,128)(2,1)} %bitcast.8, bf16[512,2560]{1,0:T(8,128)(2,1)} %weights_ref.1, bf16[1024,512]{1,0:T(8,128)(2,1)} %upstream_ref.1), custom_call_target="tpu_custom_call" | custom-call | flops 30000001024 | bytes 12000000 | tf_op jit(solution)/shard_map/layer_step/pallas_call | solution.py:348
  85.7 0.0 collective-permute-start
  85.7 3.2 %collective-permute-done.got_ref = bf16[512,1280]{1,0:T(8,128)(2,1)S(1)} collective-permute-done((bf16[512,1280]{1,0:T(8,128)(2,1)}, bf16[512,1280]{1,0:T(8,128)(2,1)S(1)}, u32[]{:S(2)}, u32[]{:S(2)}) %collective-permute-start) | collective-permute-done | bytes 1310752 | tf_op jit(solution)/shard_map/ppermute | solution.py:398
  89.0 0.0 copy-start
  89.0 1.3 copy-done
  90.3 0.0 copy-start.1
  90.3 1.2 copy-done.1
  91.5 0.5 pack_rows.1
  92.0 0.0 copy-start.2
  92.1 0.0 copy-start.3
  92.1 0.0 copy-start.4
  92.1 36.9 %all_to_all.11.arrived_ref = bf16[128,8,1152]{2,1,0:T(8,128)(2,1)S(1)} all-to-all(bf16[128,8,1152]{2,1,0:T(8,128)(2,1)S(1)} %pack_rows.1), channel_id=1, replica_groups=mesh['dp_0'=4,'dp_1'=4,'dp_2'=4,'dp_3'=2] {'dp_0','dp_1','dp_2','dp_3'}, dimensions={0} | all-to-all | bytes 4718592 | tf_op jit(solution)/shard_map/all_to_all | solution.py:393
  128.9 0.0 copy-done.2
  128.9 0.0 copy-done.3
  128.9 0.0 copy-done.4
  129.0 3.4 %finish_step.1 = (bf16[1024,512]{1,0:T(8,128)(2,1)}, f32[4,2048]{1,0:T(4,128)}, f32[4,512]{1,0:T(4,128)}) custom-call(s32[1,1024]{1,0:T(1,128)S(1)} %bitcast.7, bf16[128,8,1152]{2,1,0:T(8,128)(2,1)S(1)} %all_to_all.11.arrived_ref, f32[4,2048]{1,0:T(4,128)S(1)} %copy-done.2, f32[4,512]{1,0:T(4,128)S(1)} %copy-done.3), custom_call_target="tpu_custom_call" | custom-call | flops 1073741824 | bytes 2097152 | tf_op jit(solution)/shard_map/finish_step/pallas_call | solution.py:327
Async XLA Ops:
  85.7 3.2 %collective-permute-start = (bf16[512,1280]{1,0:T(8,128)(2,1)}, bf16[512,1280]{1,0:T(8,128)(2,1)S(1)}, u32[]{:S(2)}, u32[]{:S(2)}) collective-permute-start(bf16[512,1280]{1,0:T(8,128)(2,1)} %get-tuple-element.8), channel_id=1, source_target_pairs={{0,1},{1,0},{2,3},{3,2},{4,5},{5,4},{6,7},{7,6},{8,9},{9,8},{10,11... | collective-permute-start | bytes 3932168 | tf_op jit(solution)/shard_map/ppermute | solution.py:398
  89.0 1.3 copy-start
  90.3 1.2 copy-start.1
  92.0 36.9 %copy-start.2 = (f32[4,2048]{1,0:T(4,128)S(1)}, f32[4,2048]{1,0:T(4,128)}, u32[]{:S(2)}) copy-start(f32[4,2048]{1,0:T(4,128)} %in_ref.1) | copy-start | bytes 98308
  92.1 36.9 %copy-start.3 = (f32[4,512]{1,0:T(4,128)S(1)}, f32[4,512]{1,0:T(4,128)}, u32[]{:S(2)}) copy-start(f32[4,512]{1,0:T(4,128)} %out_ref.1) | copy-start | bytes 24580
  92.1 36.9 %copy-start.4 = (s32[1024]{0:T(1024)S(1)}, s32[1024]{0:T(1024)}, u32[]{:S(2)}) copy-start(s32[1024]{0:T(1024)} %param.9) | copy-start | bytes 12292

commit v2 on v1

--- a/solution.py
+++ b/solution.py
@@ -98,10 +98,8 @@
     attended,
     mixed_t,
     att_grad,
-    near_w,
-    near_d,
-    far_w,
-    far_d,
+    weights_kept,
+    slopes_kept,
     key_sum,
     val_sum,
     hidden_grad,
@@ -124,7 +122,7 @@
             columns = slice(g * width, (g + 1) * width)
             half = dot(tokens, weights_ref[:, columns]) * 0.5
             value, slope2 = silu_parts(half)
-            slope[rows, columns] = 0.5 * slope2
+            slope[rows, columns] = (0.5 * slope2).astype(BF)
             if g == 0:
                 gate[rows, :] = value
             elif g == 1:
@@ -134,32 +132,71 @@
             else:
                 keys[rows, :] = value.astype(BF)
 
+    offsets = [sum(TILE * (t + 1) for t in range(i)) for i in range(tiles)]
+
+    def forward_tile(p, i, low, high, edge):
+        lanes = pl.ds(pl.multiple_of(p * 128, 128), 128)
+        rows = slice(i * TILE, (i + 1) * TILE)
+        kept = slice(offsets[i] + low, offsets[i] + high)
+        stacked = two_heads(queries[rows, lanes])
+        weight, slope2 = silu_parts(dot_nt(stacked, keys[low:high, lanes]))
+        if edge:
+            place = lax.broadcasted_iota(jnp.int32, (TILE, high - low), 0) + (i * TILE - low)
+            seen = lax.broadcasted_iota(jnp.int32, (TILE, high - low), 1) <= place
+            seen = jnp.concatenate([seen, seen], axis=0)
+            weight = jnp.where(seen, weight, 0.0)
+            slope2 = jnp.where(seen, slope2, 0.0)
+        weight = weight.astype(BF)
+        weights_kept[p, :, kept] = weight
+        slopes_kept[p, :, kept] = slope2.astype(BF)
+        return rows, lanes, own_lanes(dot(weight, vals[low:high, lanes]))
+
     @pl.loop(0, pairs)
     def _(p):
-        lanes = pl.ds(pl.multiple_of(p * 128, 128), 128)
+        for i in range(tiles):
+            rows, lanes, part = forward_tile(p, i, i * TILE // BLK * BLK, (i + 1) * TILE, True)
+            attended[rows, lanes] = part
+
+    @pl.when(joined)
+    def _():
+        @pl.loop(0, pairs)
+        def _(p):
+            for i in range(BLK // TILE, tiles):
+                rows, lanes, part = forward_tile(p, i, 0, BLK, False)
+                attended[rows, lanes] += part
+
+    def backward_pair(p, reach):
+        start = pl.multiple_of(p * 128, 128)
+        lanes = pl.ds(start, 128)
+        key_sum[...] = jnp.zeros_like(key_sum)
+        val_sum[...] = jnp.zeros_like(val_sum)
         for i in range(tiles):
             rows = slice(i * TILE, (i + 1) * TILE)
             stacked = two_heads(queries[rows, lanes])
-            low, high = (i * TILE) // BLK * BLK, (i + 1) * TILE
-            span = high - low
-            weight, slope2 = silu_parts(dot_nt(stacked, keys[low:high, lanes]))
-            place = lax.broadcasted_iota(jnp.int32, (TILE, span), 0) + (i * TILE - low)
-            seen = lax.broadcasted_iota(jnp.int32, (TILE, span), 1) <= place
-            seen = jnp.concatenate([seen, seen], axis=0)
-            weight = jnp.where(seen, weight, 0.0).astype(BF)
-            near_w[p, i, :, :span] = weight
-            near_d[p, i, :, :span] = jnp.where(seen, slope2, 0.0).astype(BF)
-            attended[rows, lanes] = own_lanes(dot(weight, vals[low:high, lanes]))
-            if low > 0:
-
-                @pl.when(joined)
-                def _(i=i, rows=rows, stacked=stacked, low=low):
-                    weight, slope2 = silu_parts(dot_nt(stacked, keys[:low, lanes]))
-                    weight = weight.astype(BF)
-                    j = i - low // TILE
-                    far_w[p, j] = weight
-                    far_d[p, j] = slope2.astype(BF)
-                    attended[rows, lanes] += own_lanes(dot(weight, vals[:low, lanes]))
+            down = two_heads(att_grad[rows, lanes])
+            low, high = (0 if reach else (i * TILE) // BLK * BLK), (i + 1) * TILE
+            kept = slice(offsets[i] + low, offsets[i] + high)
+            score = dot_nt(down, vals[low:high, lanes]).astype(BF) * slopes_kept[p, :, kept]
+            val_sum[:, low:high] += dot(down.T, weights_kept[p, :, kept])
+            key_sum[:, low:high] += dot(stacked.T, score)
+            attended[rows, :128] = own_lanes(dot(score, keys[low:high, lanes]))
+        for source, group, factor in (
+            (val_sum[...].T, 1, 1.0),
+            (attended[:, :128], 2, 0.0625),
+            (key_sum[...].T, 3, 1.0),
+        ):
+            columns = pl.ds(pl.multiple_of(start + group * width, 128), 128)
+            rounded = (source * factor).astype(BF).astype(F32)
+            hidden_grad[:, columns] = (rounded * slope[:, columns].astype(F32)).astype(BF)
+
+    def over_pairs(step):
+        @pl.when(joined)
+        def _():
+            pl.loop(0, pairs)(lambda p: step(p, True))
+
+        @pl.when(jnp.logical_not(joined))
+        def _():
+            pl.loop(0, pairs)(lambda p: step(p, False))
 
     @pl.loop(0, tiles)
     def _(i):
@@ -173,43 +210,13 @@
         gates = gate[rows, :]
         mixed_t[:, rows] = (normed * gates).astype(BF).T
         mixed_grad = dot_nt(upstream_ref[rows, :], weights_ref[:, 4 * width :])
-        hidden_grad[rows, :width] = (mixed_grad * normed * slope[rows, :width]).astype(BF)
+        hidden_grad[rows, :width] = (mixed_grad * normed * slope[rows, :width].astype(F32)).astype(BF)
         down = mixed_grad * gates
         mean_down = jnp.mean(down, axis=1, keepdims=True)
         mean_both = jnp.mean(down * normed, axis=1, keepdims=True)
         att_grad[rows, :] = (scale * (down - mean_down - normed * mean_both)).astype(BF)
 
-    @pl.loop(0, pairs)
-    def _(p):
-        start = pl.multiple_of(p * 128, 128)
-        lanes = pl.ds(start, 128)
-        key_sum[...] = jnp.zeros_like(key_sum)
-        val_sum[...] = jnp.zeros_like(val_sum)
-        query_lanes = pl.ds(pl.multiple_of(start + 2 * width, 128), 128)
-        for i in range(tiles):
-            rows = slice(i * TILE, (i + 1) * TILE)
-            stacked = two_heads(queries[rows, lanes])
-            down = two_heads(att_grad[rows, lanes])
-            low, high = (i * TILE) // BLK * BLK, (i + 1) * TILE
-            span = high - low
-            score = dot_nt(down, vals[low:high, lanes]).astype(BF) * near_d[p, i, :, :span]
-            val_sum[low:high] += dot_tn(near_w[p, i, :, :span], down)
-            key_sum[low:high] += dot_tn(score, stacked)
-            attended[rows, :128] = own_lanes(dot(score, keys[low:high, lanes]))
-            if low > 0:
-
-                @pl.when(joined)
-                def _(i=i, rows=rows, stacked=stacked, down=down, low=low):
-                    j = i - low // TILE
-                    score = dot_nt(down, vals[:low, lanes]).astype(BF) * far_d[p, j]
-                    val_sum[:low] += dot_tn(far_w[p, j], down)
-                    key_sum[:low] += dot_tn(score, stacked)
-                    attended[rows, :128] += own_lanes(dot(score, keys[:low, lanes]))
-
-        for source, group, factor in ((val_sum, 1, 1.0), (attended, 2, 0.0625), (key_sum, 3, 1.0)):
-            columns = pl.ds(pl.multiple_of(start + group * width, 128), 128)
-            rounded = (source[:, :128] * factor).astype(BF).astype(F32)
-            hidden_grad[:, columns] = (rounded * slope[:, columns]).astype(BF)
+    over_pairs(backward_pair)
 
     @pl.loop(0, tiles)
     def _(i):
@@ -344,7 +351,8 @@
 
 def layer(lens, dest, inbox, weights, upstream):
     count, width = inbox.shape
-    tiles, pairs, far = count // TILE, width // 128, (count - BLK) // TILE
+    tiles, pairs = count // TILE, width // 128
+    kept = TILE * tiles * (tiles + 1) // 2
     return pl.pallas_call(
         layer_kernel,
         name="layer_step",
@@ -358,7 +366,7 @@
         scratch_shapes=[
             pltpu.VMEM((count, 128), jnp.int32),
             pltpu.VMEM((width, count), BF),
-            pltpu.VMEM((count, 4 * width), F32),
+            pltpu.VMEM((count, 4 * width), BF),
             pltpu.VMEM((count, width), F32),
             pltpu.VMEM((count, width), BF),
             pltpu.VMEM((count, width), BF),
@@ -366,16 +374,14 @@
             pltpu.VMEM((count, width), F32),
             pltpu.VMEM((width, count), BF),
             pltpu.VMEM((count, width), BF),
-            pltpu.VMEM((pairs, tiles, 2 * TILE, BLK), BF),
-            pltpu.VMEM((pairs, tiles, 2 * TILE, BLK), BF),
-            pltpu.VMEM((pairs, far, 2 * TILE, BLK), BF),
-            pltpu.VMEM((pairs, far, 2 * TILE, BLK), BF),
-            pltpu.VMEM((count, 128), F32),
-            pltpu.VMEM((count, 128), F32),
+            pltpu.VMEM((pairs, 2 * TILE, kept), BF),
+            pltpu.VMEM((pairs, 2 * TILE, kept), BF),
+            pltpu.VMEM((128, count), F32),
+            pltpu.VMEM((128, count), F32),
             pltpu.VMEM((count, 4 * width), BF),
             pltpu.VMEM((count, width), BF),
         ],
-        compiler_params=pltpu.CompilerParams(vmem_limit_bytes=60 << 20),
+        compiler_params=pltpu.CompilerParams(vmem_limit_bytes=44 << 20),
         cost_estimate=pl.CostEstimate(
             flops=30_000_000_000, bytes_accessed=12_000_000, transcendentals=10_000_000
         ),

time: 133 us -> 120 us (0.902)
  Pallas kernels: 58.1 us -> 38.5 us
  blocking collectives: 67.8 us -> 75.1 us
    pallas_call x1, Pallas kernels: 50.2 us -> 30.4 us  [layer(): pl.pallas_call(layer_kernel, name='layer_step', out_shape=(jax.ShapeDtype...]
    all_to_all x2, blocking collectives: 67.8 us -> 75.1 us  [exchange(): return lax.all_to_all(blocks, DP, split_axis=0, concat_axis=0, tiled=True)]
where the time goes in v2:
time: 120 us; the launch traced here: 119 us
  blocking collectives  75.1 us (63%)
  Pallas kernels  38.5 us (32%)
  waiting for transfers between devices  2.66 us (2%)
  local copies, waits for them, and re-layouts  1.25 us (1%)
    all_to_all x2, blocking collectives, exchange(): return lax.all_to_all(blocks, DP, split_axis=0, concat_axis=0, tiled=True)  75.1 us
    pallas_call x1, Pallas kernels, layer(): pl.pallas_call(layer_kernel, name='layer_step', out_shape=(jax.ShapeDtype...  30.4 us
    pallas_call x1, Pallas kernels, place(): pl.pallas_call(place_kernel, name='place_rows', out_shape=jax.ShapeDtypeS...  4.11 us
    pallas_call x1, Pallas kernels, finish(): pl.pallas_call(functools.partial(finish_kernel, scale), name='finish_step...  3.39 us
    ppermute x1, waiting for transfers between devices, shards(): got = lax.ppermute(given, CORE, [(0, 1), (1, 0)])  2.66 us
  transfers between devices with their start and end apart: 1, of which 1 were waited for; matrix products, arithmetic and copies ran while one was open for 0% of the time, Pallas kernels for 0%

profile of v2, /device:TPU:1, one launch (start us, length us, event | category | flops | bytes accessed | tf_op | source)
XLA Modules:
  0.0 119.2 jit_solution(12017724443455604675)
XLA Ops:
  0.6 0.0 copy-start
  0.6 0.0 copy-start.4
  0.7 0.0 copy-start.6
  0.7 4.1 %place_rows.1 = bf16[1024,512]{1,0:T(8,128)(2,1)} custom-call(s32[1,1024]{1,0:T(1,128)} %bitcast.8, bf16[1024,512]{1,0:T(8,128)(2,1)} %rows_ref.1), custom_call_target="tpu_custom_call" | custom-call | flops 1073741824 | bytes 2097152 | tf_op jit(solution)/shard_map/place_rows/pallas_call | solution.py:304
  4.8 30.9 %all_to_all.10 = bf16[128,8,512]{2,1,0:T(8,128)(2,1)S(1)} all-to-all(bf16[128,8,512]{2,1,0:T(8,128)(2,1)} %bitcast.10), channel_id=1, replica_groups=mesh['dp_0'=4,'dp_1'=4,'dp_2'=4,'dp_3'=2] {'dp_0','dp_1','dp_2','dp_3'}, dimensions={0} | all-to-all | bytes 2097152 | tf_op jit(solution)/shard_map/all_to_all | solution.py:399
  35.6 0.0 copy-done
  35.6 0.0 copy-done.4
  35.6 0.0 copy-done.6
  35.6 0.0 copy-start.1
  35.6 1.2 %copy-done.1 = bf16[1024,512]{1,0:T(8,128)(2,1)S(1)} copy-done((bf16[1024,512]{1,0:T(8,128)(2,1)S(1)}, bf16[1024,512]{1,0:T(8,128)(2,1)}, u32[]{:S(2)}) %copy-start.1) | copy-done | bytes 1048600
  36.9 30.4 %layer_step.1 = (bf16[1024,512]{1,0:T(8,128)(2,1)S(1)}, bf16[512,1280]{1,0:T(8,128)(2,1)S(1)}, bf16[512,1280]{1,0:T(8,128)(2,1)S(1)}) custom-call(s32[2]{0:T(128)S(1)} %copy-done.6, s32[1,1024]{1,0:T(1,128)S(1)} %bitcast.7, bf16[1024,512]{1,0:T(8,128)(2,1)S(1)} %bitcast.5, bf16[512,2560]{1,0:T(8,128)(2,1)S(1)} %copy-done, bf16[1024,512]{1,0:T(8,128)(2,1)S(1)} %copy-done.1), custom_call_target="tpu_custom_call" | custom-call | flops 30000001024 | bytes 12000000 | tf_op jit(solution)/shard_map/layer_step/pallas_call | solution.py:356
  67.3 1.0 collective-permute-start
  68.3 2.7 %collective-permute-done.got_ref = bf16[512,1280]{1,0:T(8,128)(2,1)S(1)} collective-permute-done((bf16[512,1280]{1,0:T(8,128)(2,1)S(1)}, bf16[512,1280]{1,0:T(8,128)(2,1)S(1)}, u32[]{:S(2)}, u32[]{:S(2)}) %collective-permute-start) | collective-permute-done | bytes 1310752 | tf_op jit(solution)/shard_map/ppermute | solution.py:404
  70.9 0.5 pack_rows.1
  71.5 0.0 copy-start.2
  71.5 0.0 copy-start.3
  71.5 0.0 copy-start.5
  71.5 44.3 %all_to_all.11.arrived_ref = bf16[128,8,1152]{2,1,0:T(8,128)(2,1)S(1)} all-to-all(bf16[128,8,1152]{2,1,0:T(8,128)(2,1)S(1)} %pack_rows.1), channel_id=1, replica_groups=mesh['dp_0'=4,'dp_1'=4,'dp_2'=4,'dp_3'=2] {'dp_0','dp_1','dp_2','dp_3'}, dimensions={0} | all-to-all | bytes 4718592 | tf_op jit(solution)/shard_map/all_to_all | solution.py:399
  115.8 0.0 copy-done.2
  115.8 0.0 copy-done.3
  115.8 0.0 copy-done.5
  115.8 3.4 %finish_step.1 = (bf16[1024,512]{1,0:T(8,128)(2,1)}, f32[4,2048]{1,0:T(4,128)}, f32[4,512]{1,0:T(4,128)}) custom-call(s32[1,1024]{1,0:T(1,128)S(1)} %bitcast.9, bf16[128,8,1152]{2,1,0:T(8,128)(2,1)S(1)} %all_to_all.11.arrived_ref, f32[4,2048]{1,0:T(4,128)S(1)} %copy-done.2, f32[4,512]{1,0:T(4,128)S(1)} %copy-done.3), custom_call_target="tpu_custom_call" | custom-call | flops 1073741824 | bytes 2097152 | tf_op jit(solution)/shard_map/finish_step/pallas_call | solution.py:334
Async XLA Ops:
  0.6 35.0 %copy-start = (bf16[512,2560]{1,0:T(8,128)(2,1)S(1)}, bf16[512,2560]{1,0:T(8,128)(2,1)}, u32[]{:S(2)}) copy-start(bf16[512,2560]{1,0:T(8,128)(2,1)} %weights_ref.1) | copy-start | bytes 7864324
  0.6 35.0 %copy-start.4 = (s32[1024]{0:T(1024)S(1)}, s32[1024]{0:T(1024)}, u32[]{:S(2)}) copy-start(s32[1024]{0:T(1024)} %param.10) | copy-start | bytes 12292
  0.7 35.0 %copy-start.6 = (s32[2]{0:T(128)S(1)}, s32[2]{0:T(128)}, u32[]{:S(2)}) copy-start(s32[2]{0:T(128)} %lens_ref.1) | copy-start | bytes 28
  35.6 1.2 %copy-start.1 = (bf16[1024,512]{1,0:T(8,128)(2,1)S(1)}, bf16[1024,512]{1,0:T(8,128)(2,1)}, u32[]{:S(2)}) copy-start(bf16[1024,512]{1,0:T(8,128)(2,1)} %upstream_ref.1) | copy-start | bytes 3145732
  67.3 3.6 %collective-permute-start = (bf16[512,1280]{1,0:T(8,128)(2,1)S(1)}, bf16[512,1280]{1,0:T(8,128)(2,1)S(1)}, u32[]{:S(2)}, u32[]{:S(2)}) collective-permute-start(bf16[512,1280]{1,0:T(8,128)(2,1)S(1)} %get-tuple-element.8), channel_id=1, source_target_pairs={{0,1},{1,0},{2,3},{3,2},{4,5},{5,4},{6,7},{7,6},{8,9},{9,8},{10,11... | collective-permute-start | bytes 3932168 | tf_op jit(solution)/shard_map/ppermute | solution.py:404
  71.5 44.3 %copy-start.2 = (f32[4,2048]{1,0:T(4,128)S(1)}, f32[4,2048]{1,0:T(4,128)}, u32[]{:S(2)}) copy-start(f32[4,2048]{1,0:T(4,128)} %in_ref.1) | copy-start | bytes 98308
  71.5 44.3 %copy-start.3 = (f32[4,512]{1,0:T(4,128)S(1)}, f32[4,512]{1,0:T(4,128)}, u32[]{:S(2)}) copy-start(f32[4,512]{1,0:T(4,128)} %out_ref.1) | copy-start | bytes 24580
  71.5 44.3 %copy-start.5 = (s32[1024]{0:T(1024)S(1)}, s32[1024]{0:T(1024)}, u32[]{:S(2)}) copy-start(s32[1024]{0:T(1024)} %param.9) | copy-start | bytes 12292

commit v3 on v2

--- a/solution.py
+++ b/solution.py
@@ -16,6 +16,7 @@
 NORM_EPS = 1e-05
 DECAY = 0.9
 TILE = 256
+WIDE = 512
 BF = jnp.bfloat16
 F32 = jnp.float32
 
@@ -32,8 +33,8 @@
     return lax.dot_general(a, b, (((0,), (0,)), ((), ())), preferred_element_type=F32)
 
 
-def rows_at(i):
-    return pl.ds(pl.multiple_of(i * TILE, TILE), TILE)
+def rows_at(i, size=TILE):
+    return pl.ds(pl.multiple_of(i * size, size), size)
 
 
 def slot_rows(slots, first, count):
@@ -85,7 +86,7 @@
     inbox_ref,
     weights_ref,
     upstream_ref,
-    sendback_ref,
+    hidden_grad,
     kept_ref,
     given_ref,
     spread_ref,
@@ -102,8 +103,6 @@
     slopes_kept,
     key_sum,
     val_sum,
-    hidden_grad,
-    token_grad,
 ):
     row_count, width = inbox_ref.shape
     tiles = row_count // TILE
@@ -112,9 +111,9 @@
     joined = jnp.where(first > 0, first, second) > BLK
     spread_ref[...] = spread_slots(dest_ref[...])
 
-    @pl.loop(0, tiles)
-    def _(i):
-        rows = rows_at(i)
+    @pl.loop(0, row_count // WIDE)
+    def _(i):
+        rows = rows_at(i, WIDE)
         pick = slot_columns(spread_ref[rows, :], row_count)
         tokens = dot(pick, inbox_ref[...]).astype(BF)
         tokens_t[:, rows] = tokens.T
@@ -139,16 +138,20 @@
         rows = slice(i * TILE, (i + 1) * TILE)
         kept = slice(offsets[i] + low, offsets[i] + high)
         stacked = two_heads(queries[rows, lanes])
-        weight, slope2 = silu_parts(dot_nt(stacked, keys[low:high, lanes]))
+        half = dot_nt(stacked, keys[low:high, lanes])
+        plus = 1.0 + jnp.tanh(half)
+        weight = (half * plus).astype(BF)
+        plus = plus.astype(BF)
+        slope2 = plus + weight * (2.0 - plus)
         if edge:
             place = lax.broadcasted_iota(jnp.int32, (TILE, high - low), 0) + (i * TILE - low)
             seen = lax.broadcasted_iota(jnp.int32, (TILE, high - low), 1) <= place
             seen = jnp.concatenate([seen, seen], axis=0)
-            weight = jnp.where(seen, weight, 0.0)
-            slope2 = jnp.where(seen, slope2, 0.0)
-        weight = weight.astype(BF)
+            none = jnp.zeros_like(weight)
+            weight = jnp.where(seen, weight, none)
+            slope2 = jnp.where(seen, slope2, none)
         weights_kept[p, :, kept] = weight
-        slopes_kept[p, :, kept] = slope2.astype(BF)
+        slopes_kept[p, :, kept] = slope2
         return rows, lanes, own_lanes(dot(weight, vals[low:high, lanes]))
 
     @pl.loop(0, pairs)
@@ -218,17 +221,6 @@
 
     over_pairs(backward_pair)
 
-    @pl.loop(0, tiles)
-    def _(i):
-        rows = rows_at(i)
-        total = dot_nt(hidden_grad[rows, :], weights_ref[:, : 4 * width])
-        token_grad[rows, :] = (upstream_ref[rows, :].astype(F32) + total).astype(BF)
-
-    @pl.loop(0, tiles)
-    def _(i):
-        pick = slot_rows(dest_ref[...], i * TILE, TILE)
-        sendback_ref[rows_at(i), :] = dot(pick, token_grad[...]).astype(BF)
-
     halves = kept_ref.shape[1] // TILE
     ours = lax.axis_index(CORE)
 
@@ -253,6 +245,21 @@
     for i in range(width // TILE):
         columns = slice(i * TILE, (i + 1) * TILE)
         put(dot(mixed_t[...], upstream_ref[:, columns]).astype(BF), inner + i)
+
+
+def back_kernel(dest_ref, hidden_grad, weights_ref, upstream_ref, sendback_ref, token_grad):
+    row_count, width = upstream_ref.shape
+
+    @pl.loop(0, row_count // WIDE)
+    def _(i):
+        rows = rows_at(i, WIDE)
+        total = dot_nt(hidden_grad[rows, :], weights_ref[:, : 4 * width])
+        token_grad[rows, :] = (upstream_ref[rows, :].astype(F32) + total).astype(BF)
+
+    @pl.loop(0, row_count // WIDE)
+    def _(i):
+        pick = slot_rows(dest_ref[...], i * WIDE, WIDE)
+        sendback_ref[rows_at(i, WIDE), :] = dot(pick, token_grad[...]).astype(BF)
 
 
 def pack_kernel(rows_ref, kept_ref, got_ref, out_ref):
@@ -311,6 +318,22 @@
             flops=2 * count * count * width, bytes_accessed=4 * count * width, transcendentals=0
         ),
     )(slots, rows)
+
+
+def back(dest, hidden_grad, weights, upstream):
+    count, width = upstream.shape
+    return pl.pallas_call(
+        back_kernel,
+        name="back_rows",
+        out_shape=jax.ShapeDtypeStruct((count, width), BF),
+        in_specs=[VMEM_SPEC] * 4,
+        out_specs=VMEM_SPEC,
+        scratch_shapes=[pltpu.VMEM((count, width), BF)],
+        compiler_params=pltpu.CompilerParams(vmem_limit_bytes=20 << 20),
+        cost_estimate=pl.CostEstimate(
+            flops=10 * count * width * width, bytes_accessed=10_000_000, transcendentals=0
+        ),
+    )(dest, hidden_grad, weights, upstream)
 
 
 def pack(rows, kept, got):
@@ -357,7 +380,7 @@
         layer_kernel,
         name="layer_step",
         out_shape=(
-            jax.ShapeDtypeStruct((count, width), BF),
+            jax.ShapeDtypeStruct((count, 4 * width), BF),
             jax.ShapeDtypeStruct((width, weights.shape[1] // 2), BF),
             jax.ShapeDtypeStruct((width, weights.shape[1] // 2), BF),
         ),
@@ -378,10 +401,8 @@
             pltpu.VMEM((pairs, 2 * TILE, kept), BF),
             pltpu.VMEM((128, count), F32),
             pltpu.VMEM((128, count), F32),
-            pltpu.VMEM((count, 4 * width), BF),
-            pltpu.VMEM((count, width), BF),
         ],
-        compiler_params=pltpu.CompilerParams(vmem_limit_bytes=44 << 20),
+        compiler_params=pltpu.CompilerParams(vmem_limit_bytes=41 << 20),
         cost_estimate=pl.CostEstimate(
             flops=30_000_000_000, bytes_accessed=12_000_000, transcendentals=10_000_000
         ),
@@ -400,8 +421,9 @@
 
     outbox = place(home, events).reshape(peers, slots, model_width)
     inbox = exchange(outbox).reshape(row_count, model_width)
-    sendback, kept, given = layer(seq_lens, dest, inbox, weights, out_grad)
+    hidden_grad, kept, given = layer(seq_lens, dest, inbox, weights, out_grad)
     got = lax.ppermute(given, CORE, [(0, 1), (1, 0)])
+    sendback = back(dest, hidden_grad, weights, out_grad)
     wire = pack(sendback.reshape(peers, slots, model_width), kept, got)
     grad_scale = (peers * row_count) ** (-0.5)
     return finish(grad_scale, home, exchange(wire), momentum_in, momentum_out)

time: 120 us -> 115 us (0.958)
  waiting for transfers between devices: 2.66 us -> 0.01 us
  Pallas kernels: 38.5 us -> 37.1 us
    pallas_call x1, Pallas kernels: 30.4 us -> 25 us  [layer(): pl.pallas_call(layer_kernel, name='layer_step', out_shape=(jax.ShapeDtype...]
    pallas_call x0 -> x1, Pallas kernels: none -> 3.98 us  [back(): pl.pallas_call(back_kernel, name='back_rows', out_shape=jax.ShapeDtypeStr...]
    ppermute x1, waiting for transfers between devices: 2.66 us -> 0.01 us  [shards(): got = lax.ppermute(given, CORE, [(0, 1), (1, 0)])]
  transfers between devices with their start and end apart: 1 -> 1, of which waited for: 1 -> 0; matrix products, arithmetic and copies ran while one was open for 0% -> 0% of each run, Pallas kernels for 0% -> 3%
where the time goes in v3:
time: 115 us
  blocking collectives  75.1 us (65%)
  Pallas kernels  37.1 us (32%)
  local copies, waits for them, and re-layouts  1.25 us (1%)
    all_to_all x2, blocking collectives, exchange(): return lax.all_to_all(blocks, DP, split_axis=0, concat_axis=0, tiled=True)  75.1 us
    pallas_call x1, Pallas kernels, layer(): pl.pallas_call(layer_kernel, name='layer_step', out_shape=(jax.ShapeDtype...  25 us
    pallas_call x1, Pallas kernels, place(): pl.pallas_call(place_kernel, name='place_rows', out_shape=jax.ShapeDtypeS...  4.12 us
    pallas_call x1, Pallas kernels, back(): pl.pallas_call(back_kernel, name='back_rows', out_shape=jax.ShapeDtypeStr...  3.98 us
    pallas_call x1, Pallas kernels, finish(): pl.pallas_call(functools.partial(finish_kernel, scale), name='finish_step...  3.39 us
  transfers between devices with their start and end apart: 1, of which 0 were waited for; matrix products, arithmetic and copies ran while one was open for 0% of the time, Pallas kernels for 3%

profile of v3, /device:TPU:1, one launch (start us, length us, event | category | flops | bytes accessed | tf_op | source)
XLA Modules:
  0.0 115.3 jit_solution(10094950721167874055)
XLA Ops:
  0.6 0.0 copy-start
  0.6 0.0 copy-start.4
  0.7 0.0 copy-start.6
  0.7 4.1 %place_rows.1 = bf16[1024,512]{1,0:T(8,128)(2,1)} custom-call(s32[1,1024]{1,0:T(1,128)} %bitcast.9, bf16[1024,512]{1,0:T(8,128)(2,1)} %rows_ref.1), custom_call_target="tpu_custom_call" | custom-call | flops 1073741824 | bytes 2097152 | tf_op jit(solution)/shard_map/place_rows/pallas_call | solution.py:311
  4.8 30.8 %all_to_all.10 = bf16[128,8,512]{2,1,0:T(8,128)(2,1)S(1)} all-to-all(bf16[128,8,512]{2,1,0:T(8,128)(2,1)} %bitcast.11), channel_id=1, replica_groups=mesh['dp_0'=4,'dp_1'=4,'dp_2'=4,'dp_3'=2] {'dp_0','dp_1','dp_2','dp_3'}, dimensions={0} | all-to-all | bytes 2097152 | tf_op jit(solution)/shard_map/all_to_all | solution.py:420
  35.6 0.0 copy-done
  35.6 0.0 copy-done.4
  35.6 0.0 copy-done.6
  35.6 0.0 copy-start.1
  35.6 1.2 %copy-done.1 = bf16[1024,512]{1,0:T(8,128)(2,1)S(1)} copy-done((bf16[1024,512]{1,0:T(8,128)(2,1)S(1)}, bf16[1024,512]{1,0:T(8,128)(2,1)}, u32[]{:S(2)}) %copy-start.1) | copy-done | bytes 1048600
  36.9 25.0 %layer_step.1 = (bf16[1024,2048]{1,0:T(8,128)(2,1)S(1)}, bf16[512,1280]{1,0:T(8,128)(2,1)S(1)}, bf16[512,1280]{1,0:T(8,128)(2,1)S(1)}) custom-call(s32[2]{0:T(128)S(1)} %copy-done.6, s32[1,1024]{1,0:T(1,128)S(1)} %bitcast.7, bf16[1024,512]{1,0:T(8,128)(2,1)S(1)} %bitcast.5, bf16[512,2560]{1,0:T(8,128)(2,1)S(1)} %copy-done, bf16[1024,512]{1,0:T(8,128)(2,1)S(1)} %copy-done.1), custom_call_target="tpu_custom_call" | custom-call | flops 30000001024 | bytes 12000000 | tf_op jit(solution)/shard_map/layer_step/pallas_call | solution.py:379
  61.9 1.1 collective-permute-start
  63.0 4.0 %back_rows.1 = bf16[1024,512]{1,0:T(8,128)(2,1)S(1)} custom-call(s32[1,1024]{1,0:T(1,128)S(1)} %bitcast.8, bf16[1024,2048]{1,0:T(8,128)(2,1)S(1)} %get-tuple-element.6.hidden_grad, bf16[512,2560]{1,0:T(8,128)(2,1)S(1)} %copy-done, bf16[1024,512]{1,0:T(8,128)(2,1)S(1)} %copy-done.1), custom_call_target="tpu_custom_call" | custom-call | flops 2684354560 | bytes 10000000 | tf_op jit(solution)/shard_map/back_rows/pallas_call | solution.py:325
  67.0 0.0 collective-permute-done.got_ref
  67.0 0.5 pack_rows.1
  67.6 0.0 copy-start.2
  67.6 0.0 copy-start.3
  67.6 0.0 copy-start.5
  67.6 44.3 %all_to_all.11.arrived_ref = bf16[128,8,1152]{2,1,0:T(8,128)(2,1)S(1)} all-to-all(bf16[128,8,1152]{2,1,0:T(8,128)(2,1)S(1)} %pack_rows.1), channel_id=1, replica_groups=mesh['dp_0'=4,'dp_1'=4,'dp_2'=4,'dp_3'=2] {'dp_0','dp_1','dp_2','dp_3'}, dimensions={0} | all-to-all | bytes 4718592 | tf_op jit(solution)/shard_map/all_to_all | solution.py:420
  111.9 0.0 copy-done.2
  111.9 0.0 copy-done.3
  111.9 0.0 copy-done.5
  111.9 3.4 %finish_step.1 = (bf16[1024,512]{1,0:T(8,128)(2,1)}, f32[4,2048]{1,0:T(4,128)}, f32[4,512]{1,0:T(4,128)}) custom-call(s32[1,1024]{1,0:T(1,128)S(1)} %bitcast.10, bf16[128,8,1152]{2,1,0:T(8,128)(2,1)S(1)} %all_to_all.11.arrived_ref, f32[4,2048]{1,0:T(4,128)S(1)} %copy-done.2, f32[4,512]{1,0:T(4,128)S(1)} %copy-done.3), custom_call_target="tpu_custom_call" | custom-call | flops 1073741824 | bytes 2097152 | tf_op jit(solution)/shard_map/finish_step/pallas_call | solution.py:357
Async XLA Ops:
  0.6 35.0 %copy-start = (bf16[512,2560]{1,0:T(8,128)(2,1)S(1)}, bf16[512,2560]{1,0:T(8,128)(2,1)}, u32[]{:S(2)}) copy-start(bf16[512,2560]{1,0:T(8,128)(2,1)} %weights_ref.3) | copy-start | bytes 7864324
  0.6 35.0 %copy-start.4 = (s32[1024]{0:T(1024)S(1)}, s32[1024]{0:T(1024)}, u32[]{:S(2)}) copy-start(s32[1024]{0:T(1024)} %param.10) | copy-start | bytes 12292
  0.7 35.0 %copy-start.6 = (s32[2]{0:T(128)S(1)}, s32[2]{0:T(128)}, u32[]{:S(2)}) copy-start(s32[2]{0:T(128)} %lens_ref.1) | copy-start | bytes 28
  35.6 1.2 %copy-start.1 = (bf16[1024,512]{1,0:T(8,128)(2,1)S(1)}, bf16[1024,512]{1,0:T(8,128)(2,1)}, u32[]{:S(2)}) copy-start(bf16[1024,512]{1,0:T(8,128)(2,1)} %upstream_ref.3) | copy-start | bytes 3145732
  61.9 5.1 %collective-permute-start = (bf16[512,1280]{1,0:T(8,128)(2,1)S(1)}, bf16[512,1280]{1,0:T(8,128)(2,1)S(1)}, u32[]{:S(2)}, u32[]{:S(2)}) collective-permute-start(bf16[512,1280]{1,0:T(8,128)(2,1)S(1)} %get-tuple-element.8), channel_id=1, source_target_pairs={{0,1},{1,0},{2,3},{3,2},{4,5},{5,4},{6,7},{7,6},{8,9},{9,8},{10,11... | collective-permute-start | bytes 3932168 | tf_op jit(solution)/shard_map/ppermute | solution.py:425
  67.6 44.3 %copy-start.2 = (f32[4,2048]{1,0:T(4,128)S(1)}, f32[4,2048]{1,0:T(4,128)}, u32[]{:S(2)}) copy-start(f32[4,2048]{1,0:T(4,128)} %in_ref.1) | copy-start | bytes 98308
  67.6 44.3 %copy-start.3 = (f32[4,512]{1,0:T(4,128)S(1)}, f32[4,512]{1,0:T(4,128)}, u32[]{:S(2)}) copy-start(f32[4,512]{1,0:T(4,128)} %out_ref.1) | copy-start | bytes 24580
  67.6 44.3 %copy-start.5 = (s32[1024]{0:T(1024)S(1)}, s32[1024]{0:T(1024)}, u32[]{:S(2)}) copy-start(s32[1024]{0:T(1024)} %param.9) | copy-start | bytes 12292

commit v4 on v3

--- a/solution.py
+++ b/solution.py
@@ -55,10 +55,10 @@
 
 
 def place_kernel(slots_ref, rows_ref, out_ref):
-    @pl.loop(0, out_ref.shape[0] // TILE)
-    def _(i):
-        pick = slot_rows(slots_ref[...], i * TILE, TILE)
-        out_ref[rows_at(i), :] = dot(pick, rows_ref[...]).astype(BF)
+    @pl.loop(0, out_ref.shape[0] // WIDE)
+    def _(i):
+        pick = slot_rows(slots_ref[...], i * WIDE, WIDE)
+        out_ref[rows_at(i, WIDE), :] = dot(pick, rows_ref[...]).astype(BF)
 
 
 def silu_parts(half):
@@ -91,7 +91,6 @@
     given_ref,
     spread_ref,
     tokens_t,
-    slope,
     gate,
     vals,
     queries,
@@ -121,7 +120,7 @@
             columns = slice(g * width, (g + 1) * width)
             half = dot(tokens, weights_ref[:, columns]) * 0.5
             value, slope2 = silu_parts(half)
-            slope[rows, columns] = (0.5 * slope2).astype(BF)
+            hidden_grad[rows, columns] = (0.5 * slope2).astype(BF)
             if g == 0:
                 gate[rows, :] = value
             elif g == 1:
@@ -190,7 +189,7 @@
         ):
             columns = pl.ds(pl.multiple_of(start + group * width, 128), 128)
             rounded = (source * factor).astype(BF).astype(F32)
-            hidden_grad[:, columns] = (rounded * slope[:, columns].astype(F32)).astype(BF)
+            hidden_grad[:, columns] = (rounded * hidden_grad[:, columns].astype(F32)).astype(BF)
 
     def over_pairs(step):
         @pl.when(joined)
@@ -213,7 +212,7 @@
         gates = gate[rows, :]
         mixed_t[:, rows] = (normed * gates).astype(BF).T
         mixed_grad = dot_nt(upstream_ref[rows, :], weights_ref[:, 4 * width :])
-        hidden_grad[rows, :width] = (mixed_grad * normed * slope[rows, :width].astype(F32)).astype(BF)
+        hidden_grad[rows, :width] = (mixed_grad * normed * hidden_grad[rows, :width].astype(F32)).astype(BF)
         down = mixed_grad * gates
         mean_down = jnp.mean(down, axis=1, keepdims=True)
         mean_both = jnp.mean(down * normed, axis=1, keepdims=True)
@@ -221,30 +220,25 @@
 
     over_pairs(backward_pair)
 
+    ours = lax.axis_index(CORE)
     halves = kept_ref.shape[1] // TILE
-    ours = lax.axis_index(CORE)
-
-    def put(value, i):
-        half = i // halves
-        columns = rows_at(i - half * halves)
-
-        @pl.when(half == ours)
-        def _():
-            kept_ref[:, columns] = value
-
-        @pl.when(half != ours)
-        def _():
-            given_ref[:, columns] = value
-
-    inner = 4 * width // TILE
-
-    @pl.loop(0, inner)
-    def _(i):
-        put(dot(tokens_t[...], hidden_grad[:, rows_at(i)]).astype(BF), i)
-
-    for i in range(width // TILE):
-        columns = slice(i * TILE, (i + 1) * TILE)
-        put(dot(mixed_t[...], upstream_ref[:, columns]).astype(BF), inner + i)
+    inner = 4 * width // TILE - halves
+
+    def write_half(half, ref):
+        @pl.loop(0, inner if half else halves)
+        def _(i):
+            columns = hidden_grad[:, rows_at(i + half * halves)]
+            ref[:, rows_at(i)] = dot(tokens_t[...], columns).astype(BF)
+
+        if half:
+            ref[:, inner * TILE :] = dot(mixed_t[...], upstream_ref[...]).astype(BF)
+
+    for core in range(2):
+
+        @pl.when(ours == core)
+        def _(core=core):
+            write_half(core, kept_ref)
+            write_half(1 - core, given_ref)
 
 
 def back_kernel(dest_ref, hidden_grad, weights_ref, upstream_ref, sendback_ref, token_grad):
@@ -281,10 +275,11 @@
     spread_ref[...] = spread_slots(slots_ref[...])
     rows_ref[...] = arrived_ref[:, :, :width].reshape(count, width)
 
-    @pl.loop(0, count // TILE)
-    def _(i):
-        pick = slot_columns(spread_ref[rows_at(i), :], count)
-        events_ref[rows_at(i), :] = dot(pick, rows_ref[...]).astype(BF)
+    @pl.loop(0, count // WIDE)
+    def _(i):
+        rows = rows_at(i, WIDE)
+        pick = slot_columns(spread_ref[rows, :], count)
+        events_ref[rows, :] = dot(pick, rows_ref[...]).astype(BF)
 
     part = arrived_ref.shape[2] - width
 
@@ -314,6 +309,7 @@
         out_shape=jax.ShapeDtypeStruct((count, width), BF),
         in_specs=[VMEM_SPEC] * 2,
         out_specs=VMEM_SPEC,
+        compiler_params=pltpu.CompilerParams(vmem_limit_bytes=12 << 20),
         cost_estimate=pl.CostEstimate(
             flops=2 * count * count * width, bytes_accessed=4 * count * width, transcendentals=0
         ),
@@ -389,7 +385,6 @@
         scratch_shapes=[
             pltpu.VMEM((count, 128), jnp.int32),
             pltpu.VMEM((width, count), BF),
-            pltpu.VMEM((count, 4 * width), BF),
             pltpu.VMEM((count, width), F32),
             pltpu.VMEM((count, width), BF),
             pltpu.VMEM((count, width), BF),
@@ -402,7 +397,7 @@
             pltpu.VMEM((128, count), F32),
             pltpu.VMEM((128, count), F32),
         ],
-        compiler_params=pltpu.CompilerParams(vmem_limit_bytes=41 << 20),
+        compiler_params=pltpu.CompilerParams(vmem_limit_bytes=37 << 20),
         cost_estimate=pl.CostEstimate(
             flops=30_000_000_000, bytes_accessed=12_000_000, transcendentals=10_000_000
         ),

time: 115 us -> 113 us (0.983)
  Pallas kernels: 37.1 us -> 33.9 us
    pallas_call x1, Pallas kernels: 4.12 us -> 1.42 us  [place(): pl.pallas_call(place_kernel, name='place_rows', out_shape=jax.ShapeDtypeS...]
  transfers between devices with their start and end apart: 1 -> 1, of which waited for: 0 -> 0; matrix products, arithmetic and copies ran while one was open for 0% -> 0% of each run, Pallas kernels for 3% -> 4%
where the time goes in v4:
time: 113 us; the launch traced here: 112 us
  blocking collectives  74.8 us (66%)
  Pallas kernels  33.9 us (30%)
  local copies, waits for them, and re-layouts  1.94 us (2%)
    all_to_all x2, blocking collectives, exchange(): return lax.all_to_all(blocks, DP, split_axis=0, concat_axis=0, tiled=True)  74.8 us
    pallas_call x1, Pallas kernels, layer(): pl.pallas_call(layer_kernel, name='layer_step', out_shape=(jax.ShapeDtype...  24.9 us
    pallas_call x1, Pallas kernels, back(): pl.pallas_call(back_kernel, name='back_rows', out_shape=jax.ShapeDtypeStr...  3.99 us
    pallas_call x1, Pallas kernels, finish(): pl.pallas_call(functools.partial(finish_kernel, scale), name='finish_step...  3.06 us
  transfers between devices with their start and end apart: 1, of which 0 were waited for; matrix products, arithmetic and copies ran while one was open for 0% of the time, Pallas kernels for 4%

profile of v4, /device:TPU:1, one launch (start us, length us, event | category | flops | bytes accessed | tf_op | source)
XLA Modules:
  0.0 112.3 jit_solution(17823054224548309315)
XLA Ops:
  0.6 0.0 copy-start.1
  0.6 1.2 %copy-done.1 = bf16[1024,512]{1,0:T(8,128)(2,1)S(1)} copy-done((bf16[1024,512]{1,0:T(8,128)(2,1)S(1)}, bf16[1024,512]{1,0:T(8,128)(2,1)}, u32[]{:S(2)}) %copy-start.1) | copy-done | bytes 1048600
  1.9 0.0 copy-start.6
  1.9 0.7 copy-done.6
  2.5 0.0 copy-start
  2.5 0.0 copy-start.2
  2.5 0.0 copy-start.5
  2.6 0.0 copy-start.8
  2.6 1.4 %place_rows.1 = bf16[1024,512]{1,0:T(8,128)(2,1)S(1)} custom-call(s32[1,1024]{1,0:T(1,128)S(1)} %bitcast.10, bf16[1024,512]{1,0:T(8,128)(2,1)S(1)} %copy-done.1), custom_call_target="tpu_custom_call" | custom-call | flops 1073741824 | bytes 2097152 | tf_op jit(solution)/shard_map/place_rows/pallas_call | solution.py:306
  4.0 30.6 %all_to_all.10 = bf16[128,8,512]{2,1,0:T(8,128)(2,1)S(1)} all-to-all(bf16[128,8,512]{2,1,0:T(8,128)(2,1)S(1)} %bitcast.6), channel_id=1, replica_groups=mesh['dp_0'=4,'dp_1'=4,'dp_2'=4,'dp_3'=2] {'dp_0','dp_1','dp_2','dp_3'}, dimensions={0} | all-to-all | bytes 2097152 | tf_op jit(solution)/shard_map/all_to_all | solution.py:415
  34.6 0.0 copy-done
  34.6 0.0 copy-done.2
  34.6 0.0 copy-done.5
  34.6 0.0 copy-done.8
  34.7 24.9 %layer_step.1 = (bf16[1024,2048]{1,0:T(8,128)(2,1)S(1)}, bf16[512,1280]{1,0:T(8,128)(2,1)S(1)}, bf16[512,1280]{1,0:T(8,128)(2,1)S(1)}) custom-call(s32[2]{0:T(128)S(1)} %copy-done.8, s32[1,1024]{1,0:T(1,128)S(1)} %bitcast.8, bf16[1024,512]{1,0:T(8,128)(2,1)S(1)} %bitcast.5, bf16[512,2560]{1,0:T(8,128)(2,1)S(1)} %copy-done, bf16[1024,512]{1,0:T(8,128)(2,1)S(1)} %copy-done.2), custom_call_target="tpu_custom_call" | custom-call | flops 30000001024 | bytes 12000000 | tf_op jit(solution)/shard_map/layer_step/pallas_call | solution.py:375
  59.5 1.0 collective-permute-start
  60.5 4.0 %back_rows.1 = bf16[1024,512]{1,0:T(8,128)(2,1)S(1)} custom-call(s32[1,1024]{1,0:T(1,128)S(1)} %bitcast.9, bf16[1024,2048]{1,0:T(8,128)(2,1)S(1)} %get-tuple-element.6.hidden_grad, bf16[512,2560]{1,0:T(8,128)(2,1)S(1)} %copy-done, bf16[1024,512]{1,0:T(8,128)(2,1)S(1)} %copy-done.2), custom_call_target="tpu_custom_call" | custom-call | flops 2684354560 | bytes 10000000 | tf_op jit(solution)/shard_map/back_rows/pallas_call | solution.py:321
  64.5 0.0 collective-permute-done.got_ref
  64.5 0.5 pack_rows.1
  65.1 0.0 copy-start.3
  65.1 0.0 copy-start.4
  65.1 0.0 copy-start.7
  65.1 44.1 %all_to_all.11.arrived_ref = bf16[128,8,1152]{2,1,0:T(8,128)(2,1)S(1)} all-to-all(bf16[128,8,1152]{2,1,0:T(8,128)(2,1)S(1)} %pack_rows.1), channel_id=1, replica_groups=mesh['dp_0'=4,'dp_1'=4,'dp_2'=4,'dp_3'=2] {'dp_0','dp_1','dp_2','dp_3'}, dimensions={0} | all-to-all | bytes 4718592 | tf_op jit(solution)/shard_map/all_to_all | solution.py:415
  109.2 0.0 copy-done.3
  109.2 0.0 copy-done.4
  109.2 0.0 copy-done.7
  109.2 3.1 %finish_step.1 = (bf16[1024,512]{1,0:T(8,128)(2,1)}, f32[4,2048]{1,0:T(4,128)}, f32[4,512]{1,0:T(4,128)}) custom-call(s32[1,1024]{1,0:T(1,128)S(1)} %bitcast.11, bf16[128,8,1152]{2,1,0:T(8,128)(2,1)S(1)} %all_to_all.11.arrived_ref, f32[4,2048]{1,0:T(4,128)S(1)} %copy-done.3, f32[4,512]{1,0:T(4,128)S(1)} %copy-done.4), custom_call_target="tpu_custom_call" | custom-call | flops 1073741824 | bytes 2097152 | tf_op jit(solution)/shard_map/finish_step/pallas_call | solution.py:353
Async XLA Ops:
  0.6 1.2 %copy-start.1 = (bf16[1024,512]{1,0:T(8,128)(2,1)S(1)}, bf16[1024,512]{1,0:T(8,128)(2,1)}, u32[]{:S(2)}) copy-start(bf16[1024,512]{1,0:T(8,128)(2,1)} %rows_ref.1) | copy-start | bytes 3145732
  1.9 0.7 copy-start.6
  2.5 32.1 %copy-start = (bf16[512,2560]{1,0:T(8,128)(2,1)S(1)}, bf16[512,2560]{1,0:T(8,128)(2,1)}, u32[]{:S(2)}) copy-start(bf16[512,2560]{1,0:T(8,128)(2,1)} %weights_ref.3) | copy-start | bytes 7864324
  2.5 32.1 %copy-start.2 = (bf16[1024,512]{1,0:T(8,128)(2,1)S(1)}, bf16[1024,512]{1,0:T(8,128)(2,1)}, u32[]{:S(2)}) copy-start(bf16[1024,512]{1,0:T(8,128)(2,1)} %upstream_ref.3) | copy-start | bytes 3145732
  2.5 32.1 %copy-start.5 = (s32[1024]{0:T(1024)S(1)}, s32[1024]{0:T(1024)}, u32[]{:S(2)}) copy-start(s32[1024]{0:T(1024)} %param.10) | copy-start | bytes 12292
  2.6 32.1 %copy-start.8 = (s32[2]{0:T(128)S(1)}, s32[2]{0:T(128)}, u32[]{:S(2)}) copy-start(s32[2]{0:T(128)} %lens_ref.1) | copy-start | bytes 28
  59.5 5.0 %collective-permute-start = (bf16[512,1280]{1,0:T(8,128)(2,1)S(1)}, bf16[512,1280]{1,0:T(8,128)(2,1)S(1)}, u32[]{:S(2)}, u32[]{:S(2)}) collective-permute-start(bf16[512,1280]{1,0:T(8,128)(2,1)S(1)} %get-tuple-element.8), channel_id=1, source_target_pairs={{0,1},{1,0},{2,3},{3,2},{4,5},{5,4},{6,7},{7,6},{8,9},{9,8},{10,11... | collective-permute-start | bytes 3932168 | tf_op jit(solution)/shard_map/ppermute | solution.py:420
  65.1 44.2 %copy-start.3 = (f32[4,2048]{1,0:T(4,128)S(1)}, f32[4,2048]{1,0:T(4,128)}, u32[]{:S(2)}) copy-start(f32[4,2048]{1,0:T(4,128)} %in_ref.1) | copy-start | bytes 98308
  65.1 44.1 %copy-start.4 = (f32[4,512]{1,0:T(4,128)S(1)}, f32[4,512]{1,0:T(4,128)}, u32[]{:S(2)}) copy-start(f32[4,512]{1,0:T(4,128)} %out_ref.1) | copy-start | bytes 24580
  65.1 44.1 %copy-start.7 = (s32[1024]{0:T(1024)S(1)}, s32[1024]{0:T(1024)}, u32[]{:S(2)}) copy-start(s32[1024]{0:T(1024)} %param.9) | copy-start | bytes 12292

commit v5 on v4

--- a/solution.py
+++ b/solution.py
@@ -42,10 +42,10 @@
     return jnp.where(slots == places, 1.0, 0.0).astype(BF)
 
 
-def slot_columns(spread, count):
+def slot_columns(spread, count, height=1.0):
     lane = lax.broadcasted_iota(jnp.int32, spread.shape, 1)
     parts = [
-        jnp.where(spread == lane + at, 1.0, 0.0).astype(BF) for at in range(0, count, 128)
+        jnp.where(spread == lane + at, height, 0.0).astype(BF) for at in range(0, count, 128)
     ]
     return jnp.concatenate(parts, axis=1)
 
@@ -113,14 +113,13 @@
     @pl.loop(0, row_count // WIDE)
     def _(i):
         rows = rows_at(i, WIDE)
-        pick = slot_columns(spread_ref[rows, :], row_count)
+        pick = slot_columns(spread_ref[rows, :], row_count, 0.5)
         tokens = dot(pick, inbox_ref[...]).astype(BF)
         tokens_t[:, rows] = tokens.T
         for g in range(4):
             columns = slice(g * width, (g + 1) * width)
-            half = dot(tokens, weights_ref[:, columns]) * 0.5
-            value, slope2 = silu_parts(half)
-            hidden_grad[rows, columns] = (0.5 * slope2).astype(BF)
+            value, slope2 = silu_parts(dot(tokens, weights_ref[:, columns]))
+            hidden_grad[rows, columns] = slope2.astype(BF)
             if g == 0:
                 gate[rows, :] = value
             elif g == 1:
@@ -139,16 +138,16 @@
         stacked = two_heads(queries[rows, lanes])
         half = dot_nt(stacked, keys[low:high, lanes])
         plus = 1.0 + jnp.tanh(half)
+        if edge:
+            place = lax.broadcasted_iota(jnp.int32, (TILE, TILE), 0)
+            seen = lax.broadcasted_iota(jnp.int32, (TILE, TILE), 1) <= place
+            seen = jnp.concatenate([seen, seen], axis=0)
+            cut = high - low - TILE
+            last = jnp.where(seen, plus[:, cut:], 0.0)
+            plus = jnp.concatenate([plus[:, :cut], last], axis=1) if cut else last
         weight = (half * plus).astype(BF)
         plus = plus.astype(BF)
         slope2 = plus + weight * (2.0 - plus)
-        if edge:
-            place = lax.broadcasted_iota(jnp.int32, (TILE, high - low), 0) + (i * TILE - low)
-            seen = lax.broadcasted_iota(jnp.int32, (TILE, high - low), 1) <= place
-            seen = jnp.concatenate([seen, seen], axis=0)
-            none = jnp.zeros_like(weight)
-            weight = jnp.where(seen, weight, none)
-            slope2 = jnp.where(seen, slope2, none)
         weights_kept[p, :, kept] = weight
         slopes_kept[p, :, kept] = slope2
         return rows, lanes, own_lanes(dot(weight, vals[low:high, lanes]))
@@ -248,7 +247,7 @@
     def _(i):
         rows = rows_at(i, WIDE)
         total = dot_nt(hidden_grad[rows, :], weights_ref[:, : 4 * width])
-        token_grad[rows, :] = (upstream_ref[rows, :].astype(F32) + total).astype(BF)
+        token_grad[rows, :] = (upstream_ref[rows, :].astype(F32) + 0.5 * total).astype(BF)
 
     @pl.loop(0, row_count // WIDE)
     def _(i):

time: 113 us -> 111 us (0.982)
  blocking collectives: 74.8 us -> 67.6 us
  Pallas kernels: 33.9 us -> 40.8 us
    all_to_all x2, blocking collectives: 74.8 us -> 67.6 us  [exchange(): return lax.all_to_all(blocks, DP, split_axis=0, concat_axis=0, tiled=True)]
    pallas_call x1, Pallas kernels: 24.9 us -> 31.8 us  [layer(): pl.pallas_call(layer_kernel, name='layer_step', out_shape=(jax.ShapeDtype...]
where the time goes in v5:
time: 111 us
  blocking collectives  67.6 us (61%)
  Pallas kernels  40.8 us (37%)
  local copies, waits for them, and re-layouts  1.94 us (2%)
    all_to_all x2, blocking collectives, exchange(): return lax.all_to_all(blocks, DP, split_axis=0, concat_axis=0, tiled=True)  67.6 us
    pallas_call x1, Pallas kernels, layer(): pl.pallas_call(layer_kernel, name='layer_step', out_shape=(jax.ShapeDtype...  31.8 us
    pallas_call x1, Pallas kernels, back(): pl.pallas_call(back_kernel, name='back_rows', out_shape=jax.ShapeDtypeStr...  3.99 us
    pallas_call x1, Pallas kernels, finish(): pl.pallas_call(functools.partial(finish_kernel, scale), name='finish_step...  3.06 us
  transfers between devices with their start and end apart: 1, of which 0 were waited for; matrix products, arithmetic and copies ran while one was open for 0% of the time, Pallas kernels for 4%

profile of v5, /device:TPU:1, one launch (start us, length us, event | category | flops | bytes accessed | tf_op | source)
XLA Modules:
  0.0 111.1 jit_solution(6774019000876495573)
XLA Ops:
  0.6 0.0 copy-start.1
  0.6 1.2 %copy-done.1 = bf16[1024,512]{1,0:T(8,128)(2,1)S(1)} copy-done((bf16[1024,512]{1,0:T(8,128)(2,1)S(1)}, bf16[1024,512]{1,0:T(8,128)(2,1)}, u32[]{:S(2)}) %copy-start.1) | copy-done | bytes 1048600
  1.9 0.0 copy-start.6
  1.9 0.7 copy-done.6
  2.5 0.0 copy-start
  2.5 0.0 copy-start.2
  2.5 0.0 copy-start.5
  2.6 0.0 copy-start.8
  2.6 1.4 %place_rows.1 = bf16[1024,512]{1,0:T(8,128)(2,1)S(1)} custom-call(s32[1,1024]{1,0:T(1,128)S(1)} %bitcast.10, bf16[1024,512]{1,0:T(8,128)(2,1)S(1)} %copy-done.1), custom_call_target="tpu_custom_call" | custom-call | flops 1073741824 | bytes 2097152 | tf_op jit(solution)/shard_map/place_rows/pallas_call | solution.py:305
  4.0 30.6 %all_to_all.10 = bf16[128,8,512]{2,1,0:T(8,128)(2,1)S(1)} all-to-all(bf16[128,8,512]{2,1,0:T(8,128)(2,1)S(1)} %bitcast.6), channel_id=1, replica_groups=mesh['dp_0'=4,'dp_1'=4,'dp_2'=4,'dp_3'=2] {'dp_0','dp_1','dp_2','dp_3'}, dimensions={0} | all-to-all | bytes 2097152 | tf_op jit(solution)/shard_map/all_to_all | solution.py:414
  34.6 0.0 copy-done
  34.6 0.0 copy-done.2
  34.6 0.0 copy-done.5
  34.6 0.0 copy-done.8
  34.7 31.8 %layer_step.1 = (bf16[1024,2048]{1,0:T(8,128)(2,1)S(1)}, bf16[512,1280]{1,0:T(8,128)(2,1)S(1)}, bf16[512,1280]{1,0:T(8,128)(2,1)S(1)}) custom-call(s32[2]{0:T(128)S(1)} %copy-done.8, s32[1,1024]{1,0:T(1,128)S(1)} %bitcast.8, bf16[1024,512]{1,0:T(8,128)(2,1)S(1)} %bitcast.5, bf16[512,2560]{1,0:T(8,128)(2,1)S(1)} %copy-done, bf16[1024,512]{1,0:T(8,128)(2,1)S(1)} %copy-done.2), custom_call_target="tpu_custom_call" | custom-call | flops 30000001024 | bytes 12000000 | tf_op jit(solution)/shard_map/layer_step/pallas_call | solution.py:374
  66.4 0.1 collective-permute-start
  66.5 4.0 %back_rows.1 = bf16[1024,512]{1,0:T(8,128)(2,1)S(1)} custom-call(s32[1,1024]{1,0:T(1,128)S(1)} %bitcast.9, bf16[1024,2048]{1,0:T(8,128)(2,1)S(1)} %get-tuple-element.6.hidden_grad, bf16[512,2560]{1,0:T(8,128)(2,1)S(1)} %copy-done, bf16[1024,512]{1,0:T(8,128)(2,1)S(1)} %copy-done.2), custom_call_target="tpu_custom_call" | custom-call | flops 2684354560 | bytes 10000000 | tf_op jit(solution)/shard_map/back_rows/pallas_call | solution.py:320
  70.5 0.0 collective-permute-done.got_ref
  70.5 0.5 pack_rows.1
  71.1 0.0 copy-start.3
  71.1 0.0 copy-start.4
  71.1 0.0 copy-start.7
  71.1 36.9 %all_to_all.11.arrived_ref = bf16[128,8,1152]{2,1,0:T(8,128)(2,1)S(1)} all-to-all(bf16[128,8,1152]{2,1,0:T(8,128)(2,1)S(1)} %pack_rows.1), channel_id=1, replica_groups=mesh['dp_0'=4,'dp_1'=4,'dp_2'=4,'dp_3'=2] {'dp_0','dp_1','dp_2','dp_3'}, dimensions={0} | all-to-all | bytes 4718592 | tf_op jit(solution)/shard_map/all_to_all | solution.py:414
  108.1 0.0 copy-done.3
  108.1 0.0 copy-done.4
  108.1 0.0 copy-done.7
  108.1 3.1 %finish_step.1 = (bf16[1024,512]{1,0:T(8,128)(2,1)}, f32[4,2048]{1,0:T(4,128)}, f32[4,512]{1,0:T(4,128)}) custom-call(s32[1,1024]{1,0:T(1,128)S(1)} %bitcast.11, bf16[128,8,1152]{2,1,0:T(8,128)(2,1)S(1)} %all_to_all.11.arrived_ref, f32[4,2048]{1,0:T(4,128)S(1)} %copy-done.3, f32[4,512]{1,0:T(4,128)S(1)} %copy-done.4), custom_call_target="tpu_custom_call" | custom-call | flops 1073741824 | bytes 2097152 | tf_op jit(solution)/shard_map/finish_step/pallas_call | solution.py:352
Async XLA Ops:
  0.6 1.2 %copy-start.1 = (bf16[1024,512]{1,0:T(8,128)(2,1)S(1)}, bf16[1024,512]{1,0:T(8,128)(2,1)}, u32[]{:S(2)}) copy-start(bf16[1024,512]{1,0:T(8,128)(2,1)} %rows_ref.1) | copy-start | bytes 3145732
  1.9 0.7 copy-start.6
  2.5 32.1 %copy-start = (bf16[512,2560]{1,0:T(8,128)(2,1)S(1)}, bf16[512,2560]{1,0:T(8,128)(2,1)}, u32[]{:S(2)}) copy-start(bf16[512,2560]{1,0:T(8,128)(2,1)} %weights_ref.3) | copy-start | bytes 7864324
  2.5 32.1 %copy-start.2 = (bf16[1024,512]{1,0:T(8,128)(2,1)S(1)}, bf16[1024,512]{1,0:T(8,128)(2,1)}, u32[]{:S(2)}) copy-start(bf16[1024,512]{1,0:T(8,128)(2,1)} %upstream_ref.3) | copy-start | bytes 3145732
  2.5 32.1 %copy-start.5 = (s32[1024]{0:T(1024)S(1)}, s32[1024]{0:T(1024)}, u32[]{:S(2)}) copy-start(s32[1024]{0:T(1024)} %param.10) | copy-start | bytes 12292
  2.6 32.1 %copy-start.8 = (s32[2]{0:T(128)S(1)}, s32[2]{0:T(128)}, u32[]{:S(2)}) copy-start(s32[2]{0:T(128)} %lens_ref.1) | copy-start | bytes 28
  66.4 4.1 %collective-permute-start = (bf16[512,1280]{1,0:T(8,128)(2,1)S(1)}, bf16[512,1280]{1,0:T(8,128)(2,1)S(1)}, u32[]{:S(2)}, u32[]{:S(2)}) collective-permute-start(bf16[512,1280]{1,0:T(8,128)(2,1)S(1)} %get-tuple-element.8), channel_id=1, source_target_pairs={{0,1},{1,0},{2,3},{3,2},{4,5},{5,4},{6,7},{7,6},{8,9},{9,8},{10,11... | collective-permute-start | bytes 3932168 | tf_op jit(solution)/shard_map/ppermute | solution.py:419
  71.1 37.0 %copy-start.3 = (f32[4,2048]{1,0:T(4,128)S(1)}, f32[4,2048]{1,0:T(4,128)}, u32[]{:S(2)}) copy-start(f32[4,2048]{1,0:T(4,128)} %in_ref.1) | copy-start | bytes 98308
  71.1 37.0 %copy-start.4 = (f32[4,512]{1,0:T(4,128)S(1)}, f32[4,512]{1,0:T(4,128)}, u32[]{:S(2)}) copy-start(f32[4,512]{1,0:T(4,128)} %out_ref.1) | copy-start | bytes 24580
  71.1 36.9 %copy-start.7 = (s32[1024]{0:T(1024)S(1)}, s32[1024]{0:T(1024)}, u32[]{:S(2)}) copy-start(s32[1024]{0:T(1024)} %param.9) | copy-start | bytes 12292

commit v6 on v5

--- a/solution.py
+++ b/solution.py
@@ -152,19 +152,13 @@
         slopes_kept[p, :, kept] = slope2
         return rows, lanes, own_lanes(dot(weight, vals[low:high, lanes]))
 
-    @pl.loop(0, pairs)
-    def _(p):
+    def forward_pair(p, reach):
         for i in range(tiles):
-            rows, lanes, part = forward_tile(p, i, i * TILE // BLK * BLK, (i + 1) * TILE, True)
+            low = i * TILE // BLK * BLK
+            rows, lanes, part = forward_tile(p, i, low, (i + 1) * TILE, True)
+            if reach and low > 0:
+                part += forward_tile(p, i, 0, low, False)[2]
             attended[rows, lanes] = part
-
-    @pl.when(joined)
-    def _():
-        @pl.loop(0, pairs)
-        def _(p):
-            for i in range(BLK // TILE, tiles):
-                rows, lanes, part = forward_tile(p, i, 0, BLK, False)
-                attended[rows, lanes] += part
 
     def backward_pair(p, reach):
         start = pl.multiple_of(p * 128, 128)
@@ -199,6 +193,8 @@
         def _():
             pl.loop(0, pairs)(lambda p: step(p, False))
 
+    over_pairs(forward_pair)
+
     @pl.loop(0, tiles)
     def _(i):
         rows = rows_at(i)

time: 111 us -> 110 us (level)
  Pallas kernels: 40.8 us -> 33.3 us
  blocking collectives: 67.6 us -> 73.1 us
    pallas_call x1, Pallas kernels: 31.8 us -> 24.3 us  [layer(): pl.pallas_call(layer_kernel, name='layer_step', out_shape=(jax.ShapeDtype...]
    all_to_all x2, blocking collectives: 67.6 us -> 73.1 us  [exchange(): return lax.all_to_all(blocks, DP, split_axis=0, concat_axis=0, tiled=True)]
where the time goes in v6:
time: 110 us
  blocking collectives  73.1 us (66%)
  Pallas kernels  33.3 us (30%)
  local copies, waits for them, and re-layouts  1.94 us (2%)
    all_to_all x2, blocking collectives, exchange(): return lax.all_to_all(blocks, DP, split_axis=0, concat_axis=0, tiled=True)  73.1 us
    pallas_call x1, Pallas kernels, layer(): pl.pallas_call(layer_kernel, name='layer_step', out_shape=(jax.ShapeDtype...  24.3 us
    pallas_call x1, Pallas kernels, back(): pl.pallas_call(back_kernel, name='back_rows', out_shape=jax.ShapeDtypeStr...  3.99 us
    pallas_call x1, Pallas kernels, finish(): pl.pallas_call(functools.partial(finish_kernel, scale), name='finish_step...  3.06 us
  transfers between devices with their start and end apart: 1, of which 0 were waited for; matrix products, arithmetic and copies ran while one was open for 0% of the time, Pallas kernels for 4%

profile of v6, /device:TPU:1, one launch (start us, length us, event | category | flops | bytes accessed | tf_op | source)
XLA Modules:
  0.0 110.0 jit_solution(8205037794139601112)
XLA Ops:
  0.6 0.0 copy-start.1
  0.6 1.2 %copy-done.1 = bf16[1024,512]{1,0:T(8,128)(2,1)S(1)} copy-done((bf16[1024,512]{1,0:T(8,128)(2,1)S(1)}, bf16[1024,512]{1,0:T(8,128)(2,1)}, u32[]{:S(2)}) %copy-start.1) | copy-done | bytes 1048600
  1.9 0.0 copy-start.6
  1.9 0.7 copy-done.6
  2.5 0.0 copy-start
  2.5 0.0 copy-start.2
  2.5 0.0 copy-start.5
  2.6 0.0 copy-start.8
  2.6 1.4 %place_rows.1 = bf16[1024,512]{1,0:T(8,128)(2,1)S(1)} custom-call(s32[1,1024]{1,0:T(1,128)S(1)} %bitcast.10, bf16[1024,512]{1,0:T(8,128)(2,1)S(1)} %copy-done.1), custom_call_target="tpu_custom_call" | custom-call | flops 1073741824 | bytes 2097152 | tf_op jit(solution)/shard_map/place_rows/pallas_call | solution.py:301
  4.0 30.6 %all_to_all.10 = bf16[128,8,512]{2,1,0:T(8,128)(2,1)S(1)} all-to-all(bf16[128,8,512]{2,1,0:T(8,128)(2,1)S(1)} %bitcast.6), channel_id=1, replica_groups=mesh['dp_0'=4,'dp_1'=4,'dp_2'=4,'dp_3'=2] {'dp_0','dp_1','dp_2','dp_3'}, dimensions={0} | all-to-all | bytes 2097152 | tf_op jit(solution)/shard_map/all_to_all | solution.py:410
  34.6 0.0 copy-done
  34.6 0.0 copy-done.2
  34.6 0.0 copy-done.5
  34.6 0.0 copy-done.8
  34.7 24.3 %layer_step.1 = (bf16[1024,2048]{1,0:T(8,128)(2,1)S(1)}, bf16[512,1280]{1,0:T(8,128)(2,1)S(1)}, bf16[512,1280]{1,0:T(8,128)(2,1)S(1)}) custom-call(s32[2]{0:T(128)S(1)} %copy-done.8, s32[1,1024]{1,0:T(1,128)S(1)} %bitcast.8, bf16[1024,512]{1,0:T(8,128)(2,1)S(1)} %bitcast.5, bf16[512,2560]{1,0:T(8,128)(2,1)S(1)} %copy-done, bf16[1024,512]{1,0:T(8,128)(2,1)S(1)} %copy-done.2), custom_call_target="tpu_custom_call" | custom-call | flops 30000001024 | bytes 12000000 | tf_op jit(solution)/shard_map/layer_step/pallas_call | solution.py:370
  58.9 1.0 collective-permute-start
  59.9 4.0 %back_rows.1 = bf16[1024,512]{1,0:T(8,128)(2,1)S(1)} custom-call(s32[1,1024]{1,0:T(1,128)S(1)} %bitcast.9, bf16[1024,2048]{1,0:T(8,128)(2,1)S(1)} %get-tuple-element.6.hidden_grad, bf16[512,2560]{1,0:T(8,128)(2,1)S(1)} %copy-done, bf16[1024,512]{1,0:T(8,128)(2,1)S(1)} %copy-done.2), custom_call_target="tpu_custom_call" | custom-call | flops 2684354560 | bytes 10000000 | tf_op jit(solution)/shard_map/back_rows/pallas_call | solution.py:316
  63.9 0.0 collective-permute-done.got_ref
  63.9 0.5 pack_rows.1
  64.5 0.0 copy-start.3
  64.5 0.0 copy-start.4
  64.5 0.0 copy-start.7
  64.5 42.4 %all_to_all.11.arrived_ref = bf16[128,8,1152]{2,1,0:T(8,128)(2,1)S(1)} all-to-all(bf16[128,8,1152]{2,1,0:T(8,128)(2,1)S(1)} %pack_rows.1), channel_id=1, replica_groups=mesh['dp_0'=4,'dp_1'=4,'dp_2'=4,'dp_3'=2] {'dp_0','dp_1','dp_2','dp_3'}, dimensions={0} | all-to-all | bytes 4718592 | tf_op jit(solution)/shard_map/all_to_all | solution.py:410
  106.9 0.0 copy-done.3
  106.9 0.0 copy-done.4
  106.9 0.0 copy-done.7
  106.9 3.1 %finish_step.1 = (bf16[1024,512]{1,0:T(8,128)(2,1)}, f32[4,2048]{1,0:T(4,128)}, f32[4,512]{1,0:T(4,128)}) custom-call(s32[1,1024]{1,0:T(1,128)S(1)} %bitcast.11, bf16[128,8,1152]{2,1,0:T(8,128)(2,1)S(1)} %all_to_all.11.arrived_ref, f32[4,2048]{1,0:T(4,128)S(1)} %copy-done.3, f32[4,512]{1,0:T(4,128)S(1)} %copy-done.4), custom_call_target="tpu_custom_call" | custom-call | flops 1073741824 | bytes 2097152 | tf_op jit(solution)/shard_map/finish_step/pallas_call | solution.py:348
Async XLA Ops:
  0.6 1.2 %copy-start.1 = (bf16[1024,512]{1,0:T(8,128)(2,1)S(1)}, bf16[1024,512]{1,0:T(8,128)(2,1)}, u32[]{:S(2)}) copy-start(bf16[1024,512]{1,0:T(8,128)(2,1)} %rows_ref.1) | copy-start | bytes 3145732
  1.9 0.7 copy-start.6
  2.5 32.1 %copy-start = (bf16[512,2560]{1,0:T(8,128)(2,1)S(1)}, bf16[512,2560]{1,0:T(8,128)(2,1)}, u32[]{:S(2)}) copy-start(bf16[512,2560]{1,0:T(8,128)(2,1)} %weights_ref.3) | copy-start | bytes 7864324
  2.5 32.1 %copy-start.2 = (bf16[1024,512]{1,0:T(8,128)(2,1)S(1)}, bf16[1024,512]{1,0:T(8,128)(2,1)}, u32[]{:S(2)}) copy-start(bf16[1024,512]{1,0:T(8,128)(2,1)} %upstream_ref.3) | copy-start | bytes 3145732
  2.5 32.1 %copy-start.5 = (s32[1024]{0:T(1024)S(1)}, s32[1024]{0:T(1024)}, u32[]{:S(2)}) copy-start(s32[1024]{0:T(1024)} %param.10) | copy-start | bytes 12292
  2.6 32.1 %copy-start.8 = (s32[2]{0:T(128)S(1)}, s32[2]{0:T(128)}, u32[]{:S(2)}) copy-start(s32[2]{0:T(128)} %lens_ref.1) | copy-start | bytes 28
  58.9 5.0 %collective-permute-start = (bf16[512,1280]{1,0:T(8,128)(2,1)S(1)}, bf16[512,1280]{1,0:T(8,128)(2,1)S(1)}, u32[]{:S(2)}, u32[]{:S(2)}) collective-permute-start(bf16[512,1280]{1,0:T(8,128)(2,1)S(1)} %get-tuple-element.8), channel_id=1, source_target_pairs={{0,1},{1,0},{2,3},{3,2},{4,5},{5,4},{6,7},{7,6},{8,9},{9,8},{10,11... | collective-permute-start | bytes 3932168 | tf_op jit(solution)/shard_map/ppermute | solution.py:415
  64.5 42.5 %copy-start.3 = (f32[4,2048]{1,0:T(4,128)S(1)}, f32[4,2048]{1,0:T(4,128)}, u32[]{:S(2)}) copy-start(f32[4,2048]{1,0:T(4,128)} %in_ref.1) | copy-start | bytes 98308
  64.5 42.5 %copy-start.4 = (f32[4,512]{1,0:T(4,128)S(1)}, f32[4,512]{1,0:T(4,128)}, u32[]{:S(2)}) copy-start(f32[4,512]{1,0:T(4,128)} %out_ref.1) | copy-start | bytes 24580
  64.5 42.5 %copy-start.7 = (s32[1024]{0:T(1024)S(1)}, s32[1024]{0:T(1024)}, u32[]{:S(2)}) copy-start(s32[1024]{0:T(1024)} %param.9) | copy-start | bytes 12292

commit v7 on v6

--- a/solution.py
+++ b/solution.py
@@ -184,16 +184,16 @@
             rounded = (source * factor).astype(BF).astype(F32)
             hidden_grad[:, columns] = (rounded * hidden_grad[:, columns].astype(F32)).astype(BF)
 
-    def over_pairs(step):
+    def over_pairs(step, unroll):
         @pl.when(joined)
         def _():
-            pl.loop(0, pairs)(lambda p: step(p, True))
+            pl.loop(0, pairs, unroll=unroll)(lambda p: step(p, True))
 
         @pl.when(jnp.logical_not(joined))
         def _():
-            pl.loop(0, pairs)(lambda p: step(p, False))
-
-    over_pairs(forward_pair)
+            pl.loop(0, pairs, unroll=unroll)(lambda p: step(p, False))
+
+    over_pairs(forward_pair, 2)
 
     @pl.loop(0, tiles)
     def _(i):
@@ -213,7 +213,7 @@
         mean_both = jnp.mean(down * normed, axis=1, keepdims=True)
         att_grad[rows, :] = (scale * (down - mean_down - normed * mean_both)).astype(BF)
 
-    over_pairs(backward_pair)
+    over_pairs(backward_pair, 1)
 
     ours = lax.axis_index(CORE)
     halves = kept_ref.shape[1] // TILE

time: 110 us -> 109 us (level)
  no operation moved by 1% of the time
where the time goes in v7:
time: 109 us; the launch traced here: 110 us
  blocking collectives  73.2 us (67%)
  Pallas kernels  32.7 us (30%)
  local copies, waits for them, and re-layouts  1.94 us (2%)
    all_to_all x2, blocking collectives, exchange(): return lax.all_to_all(blocks, DP, split_axis=0, concat_axis=0, tiled=True)  73.2 us
    pallas_call x1, Pallas kernels, layer(): pl.pallas_call(layer_kernel, name='layer_step', out_shape=(jax.ShapeDtype...  23.7 us
    pallas_call x1, Pallas kernels, back(): pl.pallas_call(back_kernel, name='back_rows', out_shape=jax.ShapeDtypeStr...  3.98 us
    pallas_call x1, Pallas kernels, finish(): pl.pallas_call(functools.partial(finish_kernel, scale), name='finish_step...  3.06 us
  transfers between devices with their start and end apart: 1, of which 0 were waited for; matrix products, arithmetic and copies ran while one was open for 0% of the time, Pallas kernels for 4%

profile of v7, /device:TPU:1, one launch (start us, length us, event | category | flops | bytes accessed | tf_op | source)
XLA Modules:
  0.0 109.5 jit_solution(4837188618043673746)
XLA Ops:
  0.6 0.0 copy-start.1
  0.6 1.2 %copy-done.1 = bf16[1024,512]{1,0:T(8,128)(2,1)S(1)} copy-done((bf16[1024,512]{1,0:T(8,128)(2,1)S(1)}, bf16[1024,512]{1,0:T(8,128)(2,1)}, u32[]{:S(2)}) %copy-start.1) | copy-done | bytes 1048600
  1.9 0.0 copy-start.6
  1.9 0.7 copy-done.6
  2.5 0.0 copy-start
  2.5 0.0 copy-start.2
  2.5 0.0 copy-start.5
  2.6 0.0 copy-start.8
  2.6 1.4 %place_rows.1 = bf16[1024,512]{1,0:T(8,128)(2,1)S(1)} custom-call(s32[1,1024]{1,0:T(1,128)S(1)} %bitcast.10, bf16[1024,512]{1,0:T(8,128)(2,1)S(1)} %copy-done.1), custom_call_target="tpu_custom_call" | custom-call | flops 1073741824 | bytes 2097152 | tf_op jit(solution)/shard_map/place_rows/pallas_call | solution.py:301
  4.0 30.6 %all_to_all.10 = bf16[128,8,512]{2,1,0:T(8,128)(2,1)S(1)} all-to-all(bf16[128,8,512]{2,1,0:T(8,128)(2,1)S(1)} %bitcast.6), channel_id=1, replica_groups=mesh['dp_0'=4,'dp_1'=4,'dp_2'=4,'dp_3'=2] {'dp_0','dp_1','dp_2','dp_3'}, dimensions={0} | all-to-all | bytes 2097152 | tf_op jit(solution)/shard_map/all_to_all | solution.py:410
  34.6 0.0 copy-done
  34.6 0.0 copy-done.2
  34.6 0.0 copy-done.5
  34.6 0.0 copy-done.8
  34.7 23.7 %layer_step.1 = (bf16[1024,2048]{1,0:T(8,128)(2,1)S(1)}, bf16[512,1280]{1,0:T(8,128)(2,1)S(1)}, bf16[512,1280]{1,0:T(8,128)(2,1)S(1)}) custom-call(s32[2]{0:T(128)S(1)} %copy-done.8, s32[1,1024]{1,0:T(1,128)S(1)} %bitcast.8, bf16[1024,512]{1,0:T(8,128)(2,1)S(1)} %bitcast.5, bf16[512,2560]{1,0:T(8,128)(2,1)S(1)} %copy-done, bf16[1024,512]{1,0:T(8,128)(2,1)S(1)} %copy-done.2), custom_call_target="tpu_custom_call" | custom-call | flops 30000001024 | bytes 12000000 | tf_op jit(solution)/shard_map/layer_step/pallas_call | solution.py:370
  58.3 1.0 collective-permute-start
  59.3 4.0 %back_rows.1 = bf16[1024,512]{1,0:T(8,128)(2,1)S(1)} custom-call(s32[1,1024]{1,0:T(1,128)S(1)} %bitcast.9, bf16[1024,2048]{1,0:T(8,128)(2,1)S(1)} %get-tuple-element.6.hidden_grad, bf16[512,2560]{1,0:T(8,128)(2,1)S(1)} %copy-done, bf16[1024,512]{1,0:T(8,128)(2,1)S(1)} %copy-done.2), custom_call_target="tpu_custom_call" | custom-call | flops 2684354560 | bytes 10000000 | tf_op jit(solution)/shard_map/back_rows/pallas_call | solution.py:316
  63.3 0.0 collective-permute-done.got_ref
  63.3 0.5 pack_rows.1
  63.9 0.0 copy-start.3
  63.9 0.0 copy-start.4
  63.9 0.0 copy-start.7
  63.9 42.6 %all_to_all.11.arrived_ref = bf16[128,8,1152]{2,1,0:T(8,128)(2,1)S(1)} all-to-all(bf16[128,8,1152]{2,1,0:T(8,128)(2,1)S(1)} %pack_rows.1), channel_id=1, replica_groups=mesh['dp_0'=4,'dp_1'=4,'dp_2'=4,'dp_3'=2] {'dp_0','dp_1','dp_2','dp_3'}, dimensions={0} | all-to-all | bytes 4718592 | tf_op jit(solution)/shard_map/all_to_all | solution.py:410
  106.4 0.0 copy-done.3
  106.4 0.0 copy-done.4
  106.4 0.0 copy-done.7
  106.5 3.1 %finish_step.1 = (bf16[1024,512]{1,0:T(8,128)(2,1)}, f32[4,2048]{1,0:T(4,128)}, f32[4,512]{1,0:T(4,128)}) custom-call(s32[1,1024]{1,0:T(1,128)S(1)} %bitcast.11, bf16[128,8,1152]{2,1,0:T(8,128)(2,1)S(1)} %all_to_all.11.arrived_ref, f32[4,2048]{1,0:T(4,128)S(1)} %copy-done.3, f32[4,512]{1,0:T(4,128)S(1)} %copy-done.4), custom_call_target="tpu_custom_call" | custom-call | flops 1073741824 | bytes 2097152 | tf_op jit(solution)/shard_map/finish_step/pallas_call | solution.py:348
Async XLA Ops:
  0.6 1.2 %copy-start.1 = (bf16[1024,512]{1,0:T(8,128)(2,1)S(1)}, bf16[1024,512]{1,0:T(8,128)(2,1)}, u32[]{:S(2)}) copy-start(bf16[1024,512]{1,0:T(8,128)(2,1)} %rows_ref.1) | copy-start | bytes 3145732
  1.9 0.7 copy-start.6
  2.5 32.1 %copy-start = (bf16[512,2560]{1,0:T(8,128)(2,1)S(1)}, bf16[512,2560]{1,0:T(8,128)(2,1)}, u32[]{:S(2)}) copy-start(bf16[512,2560]{1,0:T(8,128)(2,1)} %weights_ref.3) | copy-start | bytes 7864324
  2.5 32.1 %copy-start.2 = (bf16[1024,512]{1,0:T(8,128)(2,1)S(1)}, bf16[1024,512]{1,0:T(8,128)(2,1)}, u32[]{:S(2)}) copy-start(bf16[1024,512]{1,0:T(8,128)(2,1)} %upstream_ref.3) | copy-start | bytes 3145732
  2.5 32.1 %copy-start.5 = (s32[1024]{0:T(1024)S(1)}, s32[1024]{0:T(1024)}, u32[]{:S(2)}) copy-start(s32[1024]{0:T(1024)} %param.10) | copy-start | bytes 12292
  2.6 32.1 %copy-start.8 = (s32[2]{0:T(128)S(1)}, s32[2]{0:T(128)}, u32[]{:S(2)}) copy-start(s32[2]{0:T(128)} %lens_ref.1) | copy-start | bytes 28
  58.3 5.0 %collective-permute-start = (bf16[512,1280]{1,0:T(8,128)(2,1)S(1)}, bf16[512,1280]{1,0:T(8,128)(2,1)S(1)}, u32[]{:S(2)}, u32[]{:S(2)}) collective-permute-start(bf16[512,1280]{1,0:T(8,128)(2,1)S(1)} %get-tuple-element.8), channel_id=1, source_target_pairs={{0,1},{1,0},{2,3},{3,2},{4,5},{5,4},{6,7},{7,6},{8,9},{9,8},{10,11... | collective-permute-start | bytes 3932168 | tf_op jit(solution)/shard_map/ppermute | solution.py:415
  63.9 42.6 %copy-start.3 = (f32[4,2048]{1,0:T(4,128)S(1)}, f32[4,2048]{1,0:T(4,128)}, u32[]{:S(2)}) copy-start(f32[4,2048]{1,0:T(4,128)} %in_ref.1) | copy-start | bytes 98308
  63.9 42.6 %copy-start.4 = (f32[4,512]{1,0:T(4,128)S(1)}, f32[4,512]{1,0:T(4,128)}, u32[]{:S(2)}) copy-start(f32[4,512]{1,0:T(4,128)} %out_ref.1) | copy-start | bytes 24580
  63.9 42.6 %copy-start.7 = (s32[1024]{0:T(1024)S(1)}, s32[1024]{0:T(1024)}, u32[]{:S(2)}) copy-start(s32[1024]{0:T(1024)} %param.9) | copy-start | bytes 12292
